TPU v7x, 32 devices: a whole 2x2x4 slice. The times are simulated.
32 devices in a mesh: grp: 2 (over y), seq: 4 (over z), doc: 2 (over x), head: 2 (over core).
Axes of the slice: x: 2, y: 2, z: 4, core: 2. Of those that a mesh axis runs over, the one named last changes fastest.
Arguments:
- queries: bfloat16 [4, 1024, 4096], P(('grp', 'doc'), 'seq', 'head'), parts along dimension 0, may hold values from -13 to 13
- keys: bfloat16 [4, 1024, 2048], P(('grp', 'doc'), 'seq', 'head'), parts along dimension 0, may hold values from -13 to 13
- values: bfloat16 [4, 1024, 2048], P(('grp', 'doc'), 'seq', 'head'), parts along dimension 0, may hold values from -6 to 6
- upstream: bfloat16 [4, 1024, 4096], P(('grp', 'doc'), 'seq', 'head'), parts along dimension 0, may hold values from -6 to 6
- lengths: int32 [4, 8], P(('grp', 'doc')), parts along dimension 0, may hold values from 1 to 512, 1024 in all within a row
- layer_inputs: bfloat16 [4, 1024, 64], P(('grp', 'doc'), 'seq'), parts along dimension 0, may hold values from -6 to 6
- query_projection: bfloat16 [4096, 64], P('head'), may hold values from -0.0546875 to 0.0546875
- pair_projection: bfloat16 [2, 2048, 64], P(None, 'head'), may hold values from -0.0546875 to 0.0546875
- test_grads: bfloat16 [4096, 4096], P(('seq', 'doc', 'head')), may hold values from -0.09375 to 0.09375
- test_index: int32 [1024], replicated, may hold values from 0 to 4095
Outputs:
- doc_grads: bfloat16 [32, 4096], P(('grp', 'doc')), parts along dimension 0
- scores: float32 [32, 1024], P('grp'), parts along dimension 0
There are 2 independent parts, one for each index of `grp`. A program takes and returns all parts, laid end to end along the dimension named above; an argument that names none is the same for every part. Nothing has to cross between parts.
Inputs may be any that keep to these rules, and one draw needn't show every extreme that they name: `lengths`: each row sums to 1024, and its longest document has exactly 512 tokens.
All inputs are finite; a program needn't handle non-finite values.
Results may differ from a plain program's by a relative error of at most 0.0054.
Values may be sent and summed in bfloat16 or wider, within the bound.
A program may use at most 128 MiB of HBM per device.

v0:
```python
import functools
import math

import jax
import jax.numpy as jnp
from jax import lax
from jax.experimental import pallas as pl
from jax.experimental.pallas import tpu as pltpu
from jax.sharding import PartitionSpec as P

HEADS = 32
KV_HEADS = 16
HDIM = 128
WINDOW = 1024
QUERY_SCALE = 168
R_IN = 64
R_OUT = 64
DOCS = 8

NEG_FILL = -1e30
MESH = pl.DeviceIdType.MESH
NT = (((1,), (1,)), ((), ()))
F32 = jnp.float32
BF16 = jnp.bfloat16


def dot(a, b):
    return jnp.dot(a, b, preferred_element_type=F32)


def dot_nt(a, b):
    return lax.dot_general(a, b, NT, preferred_element_type=F32)


def doc_numbers(positions, ends):
    total = jnp.zeros(positions.shape, jnp.int32)
    for end in ends:
        total = total + (positions >= end).astype(jnp.int32)
    return total


def kernel(
    hops,
    sizes,
    lengths,
    q_hbm,
    out_hbm,
    k_hbm,
    v_hbm,
    x_ref,
    wq_ref,
    wp_ref,
    test_hbm,
    index_ref,
    low_ref,
    scores_ref,
    q_buf,
    o_buf,
    k_buf,
    v_buf,
    x_buf,
    test_buf,
    bias,
    acc_q,
    acc_kv,
    spread,
    part,
    red_in,
    red_low,
    low_all,
    own_scores,
    score_all,
    hot,
    local_sem,
    own_sem,
    ksend,
    krecv,
    vsend,
    vrecv,
    xsend,
    xrecv,
    lsend,
    lrecv,
    send1,
    recv1,
    send2,
    recv2,
    send3,
    recv3,
):
    n_seq, n_doc, n_head = sizes
    seq = lax.axis_index("seq")
    doc = lax.axis_index("doc")
    head = lax.axis_index("head")
    rows = x_ref.shape[1]
    groups = k_buf.shape[0]
    sharing = q_buf.shape[1] // (groups * HDIM)
    wide = sharing * HDIM
    extent = (hops + 1) * rows
    factor = 1.0 / math.sqrt(QUERY_SCALE)
    n_red = n_seq * n_head
    red = seq * n_head + head
    n_all = n_red * n_doc
    me = (seq * n_doc + doc) * n_head + head
    right = seq + 1
    half = rows // 2
    own_at = half + (hops - 1) * rows
    next_at = own_at + rows
    reach = next_at

    def device_of(peer):
        return {
            "seq": peer // (n_doc * n_head),
            "doc": (peer // n_head) % n_doc,
            "head": peer % n_head,
        }

    local_copies = [
        pltpu.make_async_copy(q_hbm.at[0], q_buf.at[pl.ds(0, rows)], local_sem.at[0]),
        pltpu.make_async_copy(out_hbm.at[0], o_buf.at[pl.ds(0, rows)], local_sem.at[1]),
        pltpu.make_async_copy(test_hbm, test_buf, local_sem.at[2]),
    ]
    for copy in local_copies[:2]:
        copy.start()

    barrier = pltpu.get_barrier_semaphore()

    def greet(j, carry):
        pl.semaphore_signal(
            barrier, inc=1, device_id=device_of((me + j) % n_all), device_id_type=MESH
        )
        return carry

    lax.fori_loop(1, n_all, greet, 0)

    def own_copies(g):
        cols = pl.ds(pl.multiple_of(g * HDIM, HDIM), HDIM)
        return (
            pltpu.make_async_copy(k_hbm.at[0, :, cols], k_buf.at[g, pl.ds(own_at, rows)], own_sem.at[0, g]),
            pltpu.make_async_copy(v_hbm.at[0, :, cols], v_buf.at[g, pl.ds(own_at, rows)], own_sem.at[1, g]),
        )

    def start_own(g, carry):
        for copy in own_copies(g):
            copy.start()
        return carry

    lax.fori_loop(0, groups, start_own, 0)
    local_copies[2].start()
    pl.semaphore_wait(barrier, n_all - 1)

    def hop_at(hop):
        return max(own_at - hop * rows, 0), half if hop == hops else rows

    def hop_from(hop):
        return (hop_at(hop - 1)[0] if hop > 1 else 0) + (half if hop == hops else 0)

    def pair_copies(hop, g):
        cols = pl.ds(pl.multiple_of(g * HDIM, HDIM), HDIM)
        place, size = hop_at(hop)
        source = pl.ds(hop_from(hop), size)
        copies = []
        for hbm, buf, send, recv in ((k_hbm, k_buf, ksend, krecv), (v_hbm, v_buf, vsend, vrecv)):
            copies.append(
                pltpu.make_async_remote_copy(
                    src_ref=hbm.at[0, source, cols] if hop == 1 else buf.at[g, source],
                    dst_ref=buf.at[g, pl.ds(place, size)],
                    send_sem=send.at[hop - 1, g],
                    recv_sem=recv.at[hop - 1, g],
                    device_id={"seq": right},
                    device_id_type=MESH,
                )
            )
        return copies

    def back_copies(g):
        cols = pl.ds(pl.multiple_of(g * HDIM, HDIM), HDIM)
        many = pl.ds(pl.multiple_of(g * wide, wide), wide)
        first = pl.ds(0, half)
        pieces = (
            (q_hbm.at[0, first, many], q_buf.at[pl.ds(rows, half), many]),
            (out_hbm.at[0, first, many], o_buf.at[pl.ds(rows, half), many]),
            (k_hbm.at[0, first, cols], k_buf.at[g, pl.ds(next_at, half)]),
            (v_hbm.at[0, first, cols], v_buf.at[g, pl.ds(next_at, half)]),
        )
        return [
            pltpu.make_async_remote_copy(
                src_ref=src,
                dst_ref=dst,
                send_sem=lsend.at[i, g],
                recv_sem=lrecv.at[i, g],
                device_id={"seq": seq - 1},
                device_id_type=MESH,
            )
            for i, (src, dst) in enumerate(pieces)
        ]

    def x_copy(hop):
        place, size = hop_at(hop) if hop else (next_at, half)
        source = pl.ds(hop_from(hop) if hop else 0, size)
        return pltpu.make_async_remote_copy(
            src_ref=x_buf.at[:, source] if hop > 1 else x_ref.at[:, source],
            dst_ref=x_buf.at[:, pl.ds(place, size)],
            send_sem=xsend.at[hop],
            recv_sem=xrecv.at[hop],
            device_id={"seq": right if hop else seq - 1},
            device_id_type=MESH,
        )

    def start_back(g):
        @pl.when(seq > 0)
        def _():
            for copy in back_copies(g):
                copy.start()

    def sends(hop):
        return (right < n_seq) & (seq >= hop - 1)

    def start_pair(hop, g):
        @pl.when(sends(hop))
        def _():
            for copy in pair_copies(hop, g):
                copy.start()

    for g in range(min(2, groups)):
        start_pair(1, g)
        start_back(g)

    @pl.when(sends(1))
    def _():
        x_copy(1).start()

    @pl.when(seq > 0)
    def _():
        x_copy(0).start()

    x_buf[:, own_at:next_at] = x_ref[...]

    @pl.when(seq == n_seq - 1)
    def _():
        x_buf[:, next_at:] = jnp.zeros((R_IN, half), BF16)

        def clear_next(g, carry):
            k_buf[g, next_at:] = jnp.zeros((half, HDIM), BF16)
            return carry

        lax.fori_loop(0, groups, clear_next, 0)

    for hop in range(1, hops + 1):

        @pl.when(seq < hop)
        def _(hop=hop):
            place, size = hop_at(hop)
            x_buf[:, place : place + size] = jnp.zeros((R_IN, size), BF16)

            def clear(g, carry):
                k_buf[g, place : place + size] = jnp.zeros((size, HDIM), BF16)
                v_buf[g, place : place + size] = jnp.zeros((size, HDIM), BF16)
                return carry

            lax.fori_loop(0, groups, clear, 0)

    ends = []
    for k in range(DOCS):
        ends.append(lengths[0, k] + (ends[-1] if ends else 0))
    start = seq * rows
    key_pos = start - own_at + lax.broadcasted_iota(jnp.int32, (1, extent), 1)
    key_doc = doc_numbers(key_pos, ends)
    first_key = (0, 0, half)
    for piece in range(3):
        query_pos = start + piece * half + lax.broadcasted_iota(jnp.int32, (half, 1), 0)
        query_doc = doc_numbers(query_pos, ends)
        low, high = first_key[piece], first_key[piece] + reach
        allowed = (
            (key_pos[:, low:high] <= query_pos)
            & (key_pos[:, low:high] > query_pos - WINDOW)
            & (key_pos[:, low:high] >= 0)
            & (query_doc == key_doc[:, low:high])
        )
        bias[piece] = jnp.where(allowed, 0.0, NEG_FILL)
    acc_q[...] = jnp.zeros_like(acc_q)
    acc_kv[...] = jnp.zeros_like(acc_kv)
    for copy in local_copies[:2]:
        copy.wait()

    def compute(g):
        for copy in own_copies(g):
            copy.wait()
        cols = pl.ds(pl.multiple_of(g * HDIM, HDIM), HDIM)
        many = pl.ds(pl.multiple_of(g * wide, wide), wide)
        wq = wq_ref[:, many]
        wq_stack = jnp.concatenate(
            [wq[:, h * HDIM : (h + 1) * HDIM] for h in range(sharing)], axis=0
        )
        key_proj = (dot_nt(k_buf[g], wq_stack) * factor).astype(BF16)
        wk = wp_ref[0, :, cols]
        wv = wp_ref[1, :, cols]

        def stacked(buf, piece):
            block = buf[piece * half : (piece + 1) * half, many]
            return jnp.concatenate(
                [block[:, h * HDIM : (h + 1) * HDIM] for h in range(sharing)], axis=0
            )

        def piece_backward(piece):
            low, high = first_key[piece], first_key[piece] + reach
            keys = k_buf[g, low:high]
            values = v_buf[g, low:high]
            query = stacked(q_buf, piece)
            grad_out = stacked(o_buf, piece)
            logits = dot_nt(query, keys) * factor
            logits = (logits.reshape(sharing, half, reach) + bias[piece][None]).reshape(
                sharing * half, reach
            )
            top = jnp.max(logits, axis=1, keepdims=True)
            weights = jnp.exp(logits - top)
            total = jnp.sum(weights, axis=1, keepdims=True)
            attention = weights * (1.0 / total)
            attention_grad = dot_nt(grad_out, values)
            centre = jnp.sum(attention * attention_grad, axis=1, keepdims=True)
            score_grad = (attention * (attention_grad - centre)).astype(BF16)
            attention_low = attention.astype(BF16)
            crossed = dot(score_grad, key_proj[low:high])
            for h in range(sharing):
                acc_q[piece] += crossed[
                    h * half : (h + 1) * half, h * R_OUT : (h + 1) * R_OUT
                ]
            query_proj = (dot_nt(wk, query) * factor).astype(BF16)
            out_proj = dot_nt(wv, grad_out).astype(BF16)
            acc_kv[:, low:high] += dot(query_proj, score_grad) + dot(out_proj, attention_low)

        piece_backward(1)

        @pl.when(seq < n_seq - 1)
        def _():
            piece_backward(2)

        @pl.when(seq == 0)
        def _():
            piece_backward(0)

    chosen = index_ref[...]
    tests = own_scores.shape[1]
    test_at = lax.broadcasted_iota(jnp.int32, (tests, 1), 0)
    steps = groups + hops - 1

    def build(peer, carry):
        hot[peer] = jnp.where(chosen == test_at + peer * tests, 1.0, 0.0).astype(BF16)
        return carry

    def step(it, carry):
        g = it - (hops - 1)

        @pl.when(it + 2 < groups)
        def _():
            start_pair(1, it + 2)
            start_back(it + 2)

        for hop in range(1, hops + 1):
            gg = g + hops - hop

            @pl.when((gg >= 0) & (gg < groups))
            def _(hop=hop, gg=gg):
                @pl.when(seq >= hop)
                def _():
                    for copy in pair_copies(hop, gg):
                        copy.wait_recv()

                if hop < hops:
                    start_pair(hop + 1, gg)

        @pl.when(g >= 0)
        def _():
            @pl.when(seq < n_seq - 1)
            def _():
                for copy in back_copies(g):
                    copy.wait_recv()

            compute(g)

        lax.fori_loop(it * n_all // steps, (it + 1) * n_all // steps, build, 0)
        return carry

    lax.fori_loop(0, steps, step, 0)

    for hop in range(1, hops + 1):

        @pl.when(seq >= hop)
        def _(hop=hop):
            x_copy(hop).wait_recv()

        if hop < hops:

            @pl.when(sends(hop + 1))
            def _(hop=hop):
                x_copy(hop + 1).start()

    @pl.when(seq < n_seq - 1)
    def _():
        x_copy(0).wait_recv()

    for piece in range(3):
        at = own_at + piece * half
        acc_kv[:, at : at + half] += acc_q[piece].T
    projected = acc_kv[...]
    inputs = x_buf[...]
    marked = jnp.concatenate(
        [jnp.where(key_doc == d, projected, 0.0) for d in range(DOCS)], axis=0
    )
    high = marked.astype(BF16)
    rest = (marked - high.astype(F32)).astype(BF16)
    summed = dot_nt(jnp.concatenate([high, rest], axis=0), inputs)
    spread[...] = (summed[: DOCS * R_OUT] + summed[DOCS * R_OUT :]).reshape(spread.shape)
    width = part.shape[2]
    for o in range(R_OUT):
        column = o * R_IN
        part[column // width, :, column % width : column % width + R_IN] = spread[:, o, :].astype(BF16)

    def part_copy(peer, sender, j):
        return pltpu.make_async_remote_copy(
            src_ref=part.at[peer],
            dst_ref=red_in.at[sender],
            send_sem=send1.at[j],
            recv_sem=recv1.at[sender],
            device_id={"seq": peer // n_head, "head": peer % n_head},
            device_id_type=MESH,
        )

    def send_part(j, carry):
        part_copy((red + j) % n_red, red, j).start()
        return carry

    lax.fori_loop(1, n_red, send_part, 0)
    red_in[red] = part[red]

    def take_part(j, carry):
        part_copy((red + j) % n_red, (red + j) % n_red, j).wait_recv()
        return carry

    lax.fori_loop(1, n_red, take_part, 0)
    red_low[...] = jnp.sum(red_in[...].astype(F32), axis=0).astype(BF16)

    slot = doc * n_red + red

    def slot_of(peer):
        place = device_of(peer)
        return place["doc"] * n_red + place["seq"] * n_head + place["head"]

    def low_copy(peer, sender_slot, j):
        return pltpu.make_async_remote_copy(
            src_ref=red_low,
            dst_ref=low_all.at[sender_slot],
            send_sem=send2.at[j],
            recv_sem=recv2.at[sender_slot],
            device_id=device_of(peer),
            device_id_type=MESH,
        )

    def send_low(j, carry):
        low_copy((me + j) % n_all, slot, j).start()
        return carry

    lax.fori_loop(1, n_all, send_low, 0)
    low_all[slot] = red_low[...]
    local_copies[2].wait()

    def take_low(j, carry):
        low_copy((me + j) % n_all, slot_of((me + j) % n_all), j).wait_recv()
        return carry

    lax.fori_loop(1, n_all, take_low, 0)

    local = jnp.zeros(own_scores.shape, F32)
    for i in range(n_red):
        low_ref[:, i * width : (i + 1) * width] = low_all[doc * n_red + i]
        block = jnp.concatenate(
            [low_all[d * n_red + i].astype(F32) for d in range(n_doc)], axis=0
        ).astype(BF16)
        local = local + dot_nt(block, test_buf[:, i * width : (i + 1) * width])
    own_scores[...] = local.astype(BF16)

    def score_copy(peer, sender, j):
        return pltpu.make_async_remote_copy(
            src_ref=own_scores,
            dst_ref=score_all.at[sender],
            send_sem=send3.at[j],
            recv_sem=recv3.at[sender],
            device_id=device_of(peer),
            device_id_type=MESH,
        )

    def send_score(j, carry):
        score_copy((me + j) % n_all, me, j).start()
        return carry

    lax.fori_loop(1, n_all, send_score, 0)
    score_all[me] = local.astype(BF16)
    def select(j, total):
        peer = (me + j) % n_all

        @pl.when(j > 0)
        def _():
            score_copy(peer, peer, j).wait_recv()

        return total + dot(score_all[peer], hot[peer])

    scores_ref[...] = lax.fori_loop(0, n_all, select, jnp.zeros(scores_ref.shape, F32))

    @pl.when(seq > 0)
    def _():
        x_copy(0).wait_send()

        def sent_back(g, carry):
            for copy in back_copies(g):
                copy.wait_send()
            return carry

        lax.fori_loop(0, groups, sent_back, 0)

    for hop in range(1, hops + 1):

        @pl.when(sends(hop))
        def _(hop=hop):
            x_copy(hop).wait_send()

            def sent(g, carry):
                for copy in pair_copies(hop, g):
                    copy.wait_send()
                return carry

            lax.fori_loop(0, groups, sent, 0)

    def sent_part(j, carry):
        part_copy((red + j) % n_red, red, j).wait_send()
        return carry

    lax.fori_loop(1, n_red, sent_part, 0)

    def sent_rest(j, carry):
        low_copy((me + j) % n_all, slot, j).wait_send()
        score_copy((me + j) % n_all, me, j).wait_send()
        return carry

    lax.fori_loop(1, n_all, sent_rest, 0)


def hand_over(low_in, scores_in, low_out, scores_out):
    low_out[...] = low_in[...]
    scores_out[...] = scores_in[...]


def body(
    queries,
    keys,
    values,
    upstream,
    lengths,
    layer_inputs,
    query_projection,
    pair_projection,
    test_grads,
    test_index,
):
    n_seq, n_doc, n_head = (lax.axis_size(a) for a in ("seq", "doc", "head"))
    rows = queries.shape[1]
    groups = keys.shape[2] // HDIM
    longest = (n_seq * rows) // 2
    reach = min(WINDOW, longest) - 1
    hops = min(-(-reach // rows), n_seq - 1)
    extent = (hops + 1) * rows
    half = rows // 2
    n_red = n_seq * n_head
    n_all = n_red * n_doc
    width = R_OUT * R_IN // n_red
    tests = test_grads.shape[0]
    selected = test_index.shape[0]
    vmem = pl.BlockSpec(memory_space=pltpu.VMEM)
    anywhere = pl.BlockSpec(memory_space=pl.ANY)
    dma = pltpu.SemaphoreType.DMA
    doc_low, scores = pl.pallas_call(
        functools.partial(kernel, hops, (n_seq, n_doc, n_head)),
        out_shape=(
            jax.ShapeDtypeStruct((DOCS, R_OUT * R_IN), BF16),
            jax.ShapeDtypeStruct((n_doc * DOCS, selected), F32),
        ),
        in_specs=[
            pl.BlockSpec(memory_space=pltpu.SMEM),
            anywhere,
            anywhere,
            anywhere,
            anywhere,
            vmem,
            vmem,
            vmem,
            anywhere,
            vmem,
        ],
        out_specs=(vmem, vmem),
        scratch_shapes=[
            pltpu.VMEM((rows + half, queries.shape[2]), BF16),
            pltpu.VMEM((rows + half, queries.shape[2]), BF16),
            pltpu.VMEM((groups, extent, HDIM), BF16),
            pltpu.VMEM((groups, extent, HDIM), BF16),
            pltpu.VMEM((R_IN, extent), BF16),
            pltpu.VMEM(test_grads.shape, BF16),
            pltpu.VMEM((3, half, extent - half), F32),
            pltpu.VMEM((3, half, R_OUT), F32),
            pltpu.VMEM((R_OUT, extent), F32),
            pltpu.VMEM((DOCS, R_OUT, R_IN), F32),
            pltpu.VMEM((n_red, DOCS, width), BF16),
            pltpu.VMEM((n_red, DOCS, width), BF16),
            pltpu.VMEM((DOCS, width), BF16),
            pltpu.VMEM((n_all, DOCS, width), BF16),
            pltpu.VMEM((n_doc * DOCS, tests), BF16),
            pltpu.VMEM((n_all, n_doc * DOCS, tests), BF16),
            pltpu.VMEM((n_all, tests, selected), BF16),
            dma((3,)),
            dma((2, groups)),
            dma((hops, groups)),
            dma((hops, groups)),
            dma((hops, groups)),
            dma((hops, groups)),
            dma((hops + 1,)),
            dma((hops + 1,)),
            dma((4, groups)),
            dma((4, groups)),
            dma((n_red,)),
            dma((n_red,)),
            dma((n_all,)),
            dma((n_all,)),
            dma((n_all,)),
            dma((n_all,)),
        ],
        compiler_params=pltpu.CompilerParams(
            collective_id=0, has_side_effects=True, vmem_limit_bytes=56 * 1024 * 1024
        ),
    )(
        lengths,
        queries,
        upstream,
        keys,
        values,
        layer_inputs[0].T,
        query_projection.T,
        jnp.swapaxes(pair_projection, 1, 2),
        test_grads,
        test_index.reshape(1, selected),
    )
    return pl.pallas_call(
        hand_over,
        out_shape=(
            jax.ShapeDtypeStruct(doc_low.shape, BF16),
            jax.ShapeDtypeStruct(scores.shape, F32),
        ),
        in_specs=[vmem, vmem],
        out_specs=(vmem, vmem),
    )(doc_low, scores)


def solution(mesh):
    in_specs = (
        P(("grp", "doc"), "seq", "head"),
        P(("grp", "doc"), "seq", "head"),
        P(("grp", "doc"), "seq", "head"),
        P(("grp", "doc"), "seq", "head"),
        P(("grp", "doc"), None),
        P(("grp", "doc"), "seq", None),
        P("head", None),
        P(None, "head", None),
        P(("seq", "doc", "head"), None),
        P(),
    )
    out_specs = (P(("grp", "doc"), None), P("grp", None))
    return jax.shard_map(body, mesh=mesh, in_specs=in_specs, out_specs=out_specs, check_vma=False)
```

profile of v0, /device:TPU:0, one launch (start us, length us, event | category | flops | bytes accessed | tf_op | source)
XLA Modules:
  0.0 71.9 jit_solution(16590522319286744195)
XLA Ops:
  0.6 69.8 %shard_map.113 = (bf16[8,4096]{1,0:T(8,128)(2,1)}, f32[16,1024]{1,0:T(8,128)}) custom-call(s32[1,8]{1,0:T(1,128)} %lengths.1, bf16[1,256,2048]{2,1,0:T(8,128)(2,1)} %q_hbm.1, bf16[1,256,2048]{2,1,0:T(8,128)(2,1)} %out_hbm.1, bf16[1,256,1024]{2,1,0:T(8,128)(2,1)} %k_hbm.1, bf16[1,256,1024]{2,1,0:T(8,128)(2,1)} %v_hbm.1, bf16[64,256]{1,0:T(8,128)(2,1)} %bitcast.8, ...), custom_call_target="tpu_custom_call" | custom-call | tf_op jit(solution)/shard_map/pallas_call | solution.py:580
  70.4 1.5 %shard_map.114 = (bf16[8,4096]{1,0:T(8,128)(2,1)}, f32[16,1024]{1,0:T(8,128)}) custom-call(bf16[8,4096]{1,0:T(8,128)(2,1)} %get-tuple-element.4.low_in, f32[16,1024]{1,0:T(8,128)} %get-tuple-element.5.scores_in), custom_call_target="tpu_custom_call" | custom-call | tf_op jit(solution)/shard_map/pallas_call | solution.py:649
where the time goes:
time: 72.1 us; the launch traced here: 71.9 us
  Pallas kernels  71.3 us (99%)
    pallas_call x1, Pallas kernels, body(): pl.pallas_call(functools.partial(kernel, hops, (n_seq, n_doc, n_head)), o...  69.8 us
    pallas_call x1, Pallas kernels, body(): pl.pallas_call(hand_over, out_shape=(jax.ShapeDtypeStruct(doc_low.shape,...  1.53 us

commit v1 on v0

--- a/solution.py
+++ b/solution.py
@@ -87,6 +87,8 @@
     recv2,
     send3,
     recv3,
+    up_sem,
+    down_sem,
 ):
     n_seq, n_doc, n_head = sizes
     seq = lax.axis_index("seq")
@@ -125,13 +127,21 @@
 
     barrier = pltpu.get_barrier_semaphore()
 
-    def greet(j, carry):
-        pl.semaphore_signal(
-            barrier, inc=1, device_id=device_of((me + j) % n_all), device_id_type=MESH
-        )
-        return carry
-
-    lax.fori_loop(1, n_all, greet, 0)
+    def tell(sem, place):
+        pl.semaphore_signal(sem, inc=1, device_id=place, device_id_type=MESH)
+
+    @pl.when(seq > 0)
+    def _():
+        tell(barrier, {"seq": seq - 1})
+
+    @pl.when(right < n_seq)
+    def _():
+        tell(barrier, {"seq": right})
+
+    for j in range(1, n_doc):
+        tell(barrier, {"doc": (doc + j) % n_doc})
+    for j in range(1, n_head):
+        tell(barrier, {"head": (head + j) % n_head})
 
     def own_copies(g):
         cols = pl.ds(pl.multiple_of(g * HDIM, HDIM), HDIM)
@@ -147,7 +157,8 @@
 
     lax.fori_loop(0, groups, start_own, 0)
     local_copies[2].start()
-    pl.semaphore_wait(barrier, n_all - 1)
+    near = (seq > 0).astype(jnp.int32) + (right < n_seq).astype(jnp.int32)
+    pl.semaphore_wait(barrier, n_doc + n_head - 2 + near)
 
     def hop_at(hop):
         return max(own_at - hop * rows, 0), half if hop == hops else rows
@@ -379,6 +390,27 @@
             compute(g)
 
         lax.fori_loop(it * n_all // steps, (it + 1) * n_all // steps, build, 0)
+
+        @pl.when(it == 1)
+        def _():
+            @pl.when(seq > 0)
+            def _():
+                pl.semaphore_wait(up_sem, 1)
+
+            @pl.when(right < n_seq)
+            def _():
+                tell(up_sem, {"seq": right})
+
+        @pl.when(it == 3)
+        def _():
+            @pl.when(right < n_seq)
+            def _():
+                pl.semaphore_wait(down_sem, 1)
+
+            @pl.when(seq > 0)
+            def _():
+                tell(down_sem, {"seq": seq - 1})
+
         return carry
 
     lax.fori_loop(0, steps, step, 0)
@@ -630,6 +662,8 @@
             dma((n_all,)),
             dma((n_all,)),
             dma((n_all,)),
+            pltpu.SemaphoreType.REGULAR,
+            pltpu.SemaphoreType.REGULAR,
         ],
         compiler_params=pltpu.CompilerParams(
             collective_id=0, has_side_effects=True, vmem_limit_bytes=56 * 1024 * 1024

time: 72.1 us -> 70.9 us (0.983)
  Pallas kernels: 71.3 us -> 70.1 us
    pallas_call x1, Pallas kernels: 69.8 us -> 68.5 us  [body(): pl.pallas_call(functools.partial(kernel, hops, (n_seq, n_doc, n_head)), o...]
where the time goes in v1:
time: 70.9 us; the launch traced here: 70.7 us
  Pallas kernels  70.1 us (99%)
    pallas_call x1, Pallas kernels, body(): pl.pallas_call(functools.partial(kernel, hops, (n_seq, n_doc, n_head)), o...  68.5 us
    pallas_call x1, Pallas kernels, body(): pl.pallas_call(hand_over, out_shape=(jax.ShapeDtypeStruct(doc_low.shape,...  1.53 us

profile of v1, /device:TPU:0, one launch (start us, length us, event | category | flops | bytes accessed | tf_op | source)
XLA Modules:
  0.0 70.7 jit_solution(17877980679244537583)
XLA Ops:
  0.6 68.5 %shard_map.113 = (bf16[8,4096]{1,0:T(8,128)(2,1)}, f32[16,1024]{1,0:T(8,128)}) custom-call(s32[1,8]{1,0:T(1,128)} %lengths.1, bf16[1,256,2048]{2,1,0:T(8,128)(2,1)} %q_hbm.1, bf16[1,256,2048]{2,1,0:T(8,128)(2,1)} %out_hbm.1, bf16[1,256,1024]{2,1,0:T(8,128)(2,1)} %k_hbm.1, bf16[1,256,1024]{2,1,0:T(8,128)(2,1)} %v_hbm.1, bf16[64,256]{1,0:T(8,128)(2,1)} %bitcast.8, ...), custom_call_target="tpu_custom_call" | custom-call | tf_op jit(solution)/shard_map/pallas_call | solution.py:612
  69.2 1.5 %shard_map.114 = (bf16[8,4096]{1,0:T(8,128)(2,1)}, f32[16,1024]{1,0:T(8,128)}) custom-call(bf16[8,4096]{1,0:T(8,128)(2,1)} %get-tuple-element.4.low_in, f32[16,1024]{1,0:T(8,128)} %get-tuple-element.5.scores_in), custom_call_target="tpu_custom_call" | custom-call | tf_op jit(solution)/shard_map/pallas_call | solution.py:683

commit v2 on v1

--- a/solution.py
+++ b/solution.py
@@ -576,6 +576,671 @@
     lax.fori_loop(1, n_all, sent_rest, 0)
 
 
+def pair_kernel(
+    sizes,
+    lengths,
+    q_hbm,
+    out_hbm,
+    k_hbm,
+    v_hbm,
+    x_ref,
+    wq_ref,
+    wp_ref,
+    test_hbm,
+    index_ref,
+    low_ref,
+    scores_ref,
+    q_buf,
+    o_buf,
+    k_buf,
+    v_buf,
+    near_k,
+    near_v,
+    far_k,
+    far_v,
+    pass_k,
+    pass_v,
+    next_q,
+    next_o,
+    x_buf,
+    test_buf,
+    bias_near,
+    bias_far,
+    bias_next,
+    near_work,
+    far_work,
+    home_work,
+    next_work,
+    near_stats,
+    far_stats,
+    home_stats,
+    next_stats,
+    home_rest,
+    next_rest,
+    acc_q,
+    acc_kv,
+    acc_far,
+    spread,
+    part,
+    red_in,
+    red_low,
+    low_all,
+    own_scores,
+    score_all,
+    hot,
+    local_sem,
+    own_sem,
+    nsend,
+    nrecv,
+    fsend,
+    frecv,
+    qsend,
+    qrecv,
+    xsend,
+    xrecv,
+    hsend,
+    hrecv,
+    tsend,
+    trecv,
+    send1,
+    recv1,
+    send2,
+    recv2,
+    send3,
+    recv3,
+    up_sem,
+    down_sem,
+):
+    n_seq, n_doc, n_head = sizes
+    seq = lax.axis_index("seq")
+    doc = lax.axis_index("doc")
+    head = lax.axis_index("head")
+    rows = x_ref.shape[1]
+    groups = k_buf.shape[0]
+    pairs = near_k.shape[0]
+    sharing = q_buf.shape[1] // (groups * HDIM)
+    wide = sharing * HDIM
+    factor = 1.0 / math.sqrt(QUERY_SCALE)
+    power = factor * math.log2(math.e)
+    n_red = n_seq * n_head
+    red = seq * n_head + head
+    n_all = n_red * n_doc
+    me = (seq * n_doc + doc) * n_head + head
+    right = seq + 1
+    has_left = seq > 0
+    has_right = right < n_seq
+
+    def device_of(peer):
+        return {
+            "seq": peer // (n_doc * n_head),
+            "doc": (peer // n_head) % n_doc,
+            "head": peer % n_head,
+        }
+
+    local_copies = [
+        pltpu.make_async_copy(q_hbm.at[0], q_buf, local_sem.at[0]),
+        pltpu.make_async_copy(out_hbm.at[0], o_buf, local_sem.at[1]),
+        pltpu.make_async_copy(test_hbm, test_buf, local_sem.at[2]),
+    ]
+    barrier = pltpu.get_barrier_semaphore()
+
+    def tell(sem, place):
+        pl.semaphore_signal(sem, inc=1, device_id=place, device_id_type=MESH)
+
+    @pl.when(has_left)
+    def _():
+        tell(barrier, {"seq": seq - 1})
+
+    @pl.when(has_right)
+    def _():
+        tell(barrier, {"seq": right})
+
+    for j in range(1, n_doc):
+        tell(barrier, {"doc": (doc + j) % n_doc})
+    for j in range(1, n_head):
+        tell(barrier, {"head": (head + j) % n_head})
+
+    def columns(g, size):
+        return pl.ds(pl.multiple_of(g * size, size), size)
+
+    def own_copies(g):
+        cols = columns(g, HDIM)
+        return (
+            pltpu.make_async_copy(k_hbm.at[0, :, cols], k_buf.at[g], own_sem.at[0, g]),
+            pltpu.make_async_copy(v_hbm.at[0, :, cols], v_buf.at[g], own_sem.at[1, g]),
+        )
+
+    def start_own(g, carry):
+        for copy in own_copies(g):
+            copy.start()
+        return carry
+
+    lax.fori_loop(0, groups, start_own, 0)
+    for copy in local_copies:
+        copy.start()
+    near = has_left.astype(jnp.int32) + has_right.astype(jnp.int32)
+    pl.semaphore_wait(barrier, n_doc + n_head - 2 + near)
+
+    def remote(src, dst, send, recv, place):
+        return pltpu.make_async_remote_copy(
+            src_ref=src,
+            dst_ref=dst,
+            send_sem=send,
+            recv_sem=recv,
+            device_id={"seq": place},
+            device_id_type=MESH,
+        )
+
+    def near_copies(p):
+        cols = columns(2 * p, HDIM)
+        return [
+            remote(hbm.at[0, :, cols], buf.at[p], nsend.at[i, p], nrecv.at[i, p], right)
+            for i, (hbm, buf) in enumerate(((k_hbm, near_k), (v_hbm, near_v)))
+        ]
+
+    def far_copies(p):
+        return [
+            remote(src.at[p], buf.at[p], fsend.at[i, p], frecv.at[i, p], right)
+            for i, (src, buf) in enumerate(((pass_k, far_k), (pass_v, far_v)))
+        ]
+
+    def next_copies(p):
+        many = columns(2 * p + 1, wide)
+        return [
+            remote(hbm.at[0, :, many], buf.at[p], qsend.at[i, p], qrecv.at[i, p], seq - 1)
+            for i, (hbm, buf) in enumerate(((q_hbm, next_q), (out_hbm, next_o)))
+        ]
+
+    def x_copy(i):
+        source = x_buf.at[:, rows : 2 * rows] if i == 1 else x_ref
+        at = (rows, 0, 3 * rows)[i]
+        place = seq - 1 if i == 2 else right
+        return remote(source, x_buf.at[:, at : at + rows], xsend.at[i], xrecv.at[i], place)
+
+    def home_copy(p):
+        return remote(home_stats.at[p], next_rest.at[p], hsend.at[p], hrecv.at[p], seq - 1)
+
+    def rest_copy(p):
+        return remote(next_stats.at[p], home_rest.at[p], tsend.at[p], trecv.at[p], right)
+
+    def start_pair(p):
+        @pl.when(has_right)
+        def _():
+            for copy in near_copies(p):
+                copy.start()
+
+        @pl.when(has_left)
+        def _():
+            for copy in next_copies(p):
+                copy.start()
+
+    for p in range(min(2, pairs)):
+        start_pair(p)
+
+    @pl.when(has_right)
+    def _():
+        x_copy(0).start()
+
+    @pl.when(has_left)
+    def _():
+        x_copy(2).start()
+
+    x_buf[:, 2 * rows : 3 * rows] = x_ref[...]
+
+    @pl.when(seq == 0)
+    def _():
+        x_buf[:, rows : 2 * rows] = jnp.zeros((R_IN, rows), BF16)
+        for buf in (near_k, near_v, far_k, far_v, home_rest):
+            buf[...] = jnp.zeros(buf.shape, buf.dtype)
+
+    @pl.when(seq < 2)
+    def _():
+        x_buf[:, :rows] = jnp.zeros((R_IN, rows), BF16)
+
+    @pl.when(right == n_seq)
+    def _():
+        x_buf[:, 3 * rows :] = jnp.zeros((R_IN, rows), BF16)
+        for buf in (next_q, next_o):
+            buf[...] = jnp.zeros(buf.shape, buf.dtype)
+        next_rest[...] = jnp.ones(next_rest.shape, F32)
+
+    ends = []
+    for k in range(DOCS):
+        ends.append(lengths[0, k] + (ends[-1] if ends else 0))
+    start = seq * rows
+
+    def doc_at(position):
+        total = 0
+        for end in ends:
+            total = total + (position >= end).astype(jnp.int32)
+        return total
+
+    covered = has_left & has_right & (doc_at(start - 1) == doc_at(start + rows))
+    carried = (seq > 1) & (doc_at(start - rows - 1) == doc_at(start))
+    carried_rows = carried.astype(jnp.int32) * rows
+    missing = jnp.where(covered, 0.0, NEG_FILL)
+
+    def bias_of(key_start, size, query_start):
+        key_pos = key_start + lax.broadcasted_iota(jnp.int32, (size, 1), 0)
+        query_pos = query_start + lax.broadcasted_iota(jnp.int32, (1, rows), 1)
+        allowed = (
+            (key_pos <= query_pos)
+            & (key_pos > query_pos - WINDOW)
+            & (key_pos >= 0)
+            & (doc_numbers(key_pos, ends) == doc_numbers(query_pos, ends))
+        )
+        return jnp.where(allowed, 0.0, NEG_FILL)
+
+    bias_near[...] = bias_of(start - rows, 2 * rows, start)
+    bias_far[...] = bias_of(start - rows - carried_rows, rows, start)
+    bias_next[...] = bias_of(start - rows, 2 * rows, start + rows) + missing
+    acc_q[...] = jnp.zeros_like(acc_q)
+    acc_kv[...] = jnp.zeros_like(acc_kv)
+    acc_far[...] = jnp.zeros_like(acc_far)
+    for copy in local_copies[:2]:
+        copy.wait()
+
+    def by_head(block):
+        return jnp.concatenate(
+            [block[:, h * HDIM : (h + 1) * HDIM] for h in range(sharing)], axis=0
+        )
+
+    def forward(keys, values, query, grad_out, bias, work, at, stats, p):
+        logits = dot_nt(keys, query) + jnp.concatenate([bias] * sharing, axis=1)
+        top = jnp.max(logits, axis=0, keepdims=True)
+        weights = jnp.exp2((logits - top) * power)
+        attention_grad = dot_nt(values, grad_out)
+        work[at, 0] = weights
+        work[at, 1] = attention_grad
+        stats[p, 0:1] = top
+        stats[p, 1:2] = jnp.sum(weights, axis=0, keepdims=True)
+        stats[p, 2:3] = jnp.sum(weights * attention_grad, axis=0, keepdims=True)
+
+    def rows_of(stats, p):
+        return stats[p, 0:1], stats[p, 1:2], stats[p, 2:3]
+
+    def choose(first, second):
+        return tuple(jnp.where(carried, a, b) for a, b in zip(first, second))
+
+    def share(mine, other):
+        top = jnp.maximum(mine[0], other[0])
+        my_part = jnp.exp2((mine[0] - top) * power)
+        other_part = jnp.exp2((other[0] - top) * power)
+        scale = 1.0 / (mine[1] * my_part + other[1] * other_part)
+        return my_part * scale, (mine[2] * my_part + other[2] * other_part) * scale
+
+    def project(group, query, grad_out):
+        cols = columns(group, HDIM)
+        return (
+            (dot_nt(wp_ref[0, :, cols], query) * factor).astype(BF16),
+            dot_nt(wp_ref[1, :, cols], grad_out).astype(BF16),
+        )
+
+    def key_projection(weight, keys):
+        return [
+            (dot_nt(weight[:, h * HDIM : (h + 1) * HDIM], keys) * factor).astype(BF16)
+            for h in range(sharing)
+        ]
+
+    def backward(work, at, shares, key_proj, projected, query_at):
+        scale, centre = shares
+        attention = work[at, 0] * scale
+        score_grad = (attention * (work[at, 1] - centre)).astype(BF16)
+        attention_low = attention.astype(BF16)
+        crossed = dot(key_proj[0], score_grad[:, :rows])
+        for h in range(1, sharing):
+            crossed = crossed + dot(key_proj[h], score_grad[:, h * rows : (h + 1) * rows])
+        acc_q[query_at] += crossed
+        return dot_nt(score_grad, projected[0]) + dot_nt(attention_low, projected[1])
+
+    def queries_of(g):
+        many = columns(g, wide)
+        return by_head(q_buf[:, many]), by_head(o_buf[:, many])
+
+    def first(p):
+        a, b = 2 * p, 2 * p + 1
+        for g in (a, b):
+            for copy in own_copies(g):
+                copy.wait()
+
+        @pl.when(has_left)
+        def _():
+            for copy in near_copies(p):
+                copy.wait_recv()
+
+        pass_k[p] = jnp.where(covered, near_k[p], k_buf[b])
+        pass_v[p] = jnp.where(covered, near_v[p], v_buf[b])
+
+        @pl.when(has_right)
+        def _():
+            for copy in far_copies(p):
+                copy.start()
+
+        @pl.when(p + 2 < pairs)
+        def _():
+            start_pair(p + 2)
+
+        query, grad_out = queries_of(b)
+        forward(
+            k_buf[b], v_buf[b], query, grad_out, bias_near[rows:], home_work, p, home_stats, p
+        )
+
+        @pl.when(has_left)
+        def _():
+            home_copy(p).start()
+
+        query, grad_out = queries_of(a)
+        keys = jnp.concatenate([near_k[p], k_buf[a]], axis=0)
+        values = jnp.concatenate([near_v[p], v_buf[a]], axis=0)
+        forward(keys, values, query, grad_out, bias_near[...], near_work, p, near_stats, p)
+
+    def second(p):
+        a, b = 2 * p, 2 * p + 1
+
+        @pl.when(has_left)
+        def _():
+            for copy in far_copies(p):
+                copy.wait_recv()
+
+        @pl.when(has_right)
+        def _():
+            for copy in next_copies(p):
+                copy.wait_recv()
+
+        keys = jnp.concatenate([far_k[p], k_buf[b]], axis=0)
+        values = jnp.concatenate([far_v[p], v_buf[b]], axis=0)
+        forward(
+            keys,
+            values,
+            by_head(next_q[p]),
+            by_head(next_o[p]),
+            bias_next[...],
+            next_work,
+            p,
+            next_stats,
+            p,
+        )
+
+        @pl.when(has_right)
+        def _():
+            rest_copy(p).start()
+
+        query_a, out_a = queries_of(a)
+        query_b, out_b = queries_of(b)
+        query = jnp.where(carried, query_a, query_b)
+        grad_out = jnp.where(carried, out_a, out_b)
+        forward(
+            far_k[p], far_v[p], query, grad_out, bias_far[...], far_work, 0, far_stats, p
+        )
+        mine = rows_of(near_stats, p)
+        home = rows_of(home_stats, p)
+        far = rows_of(far_stats, p)
+        none = (jnp.full_like(far[0], 2 * NEG_FILL), jnp.zeros_like(far[1]), jnp.zeros_like(far[2]))
+        weight_a, weight_b = wq_ref[:, columns(a, wide)], wq_ref[:, columns(b, wide)]
+        weight = jnp.where(carried, weight_a, weight_b)
+        project_a = project(a, query_a, out_a)
+        keys = jnp.concatenate([near_k[p], k_buf[a]], axis=0)
+        acc_kv[rows : 3 * rows] += backward(
+            near_work,
+            p,
+            share(mine, choose(far, none)),
+            key_projection(weight_a, keys),
+            project_a,
+            0,
+        )
+        project_b = project(b, query_b, out_b)
+        acc_far[...] += backward(
+            far_work,
+            0,
+            share(far, choose(mine, home)),
+            key_projection(weight, far_k[p]),
+            choose(project_a, project_b),
+            0,
+        )
+
+    def third(p):
+        b = 2 * p + 1
+
+        @pl.when(has_left)
+        def _():
+            rest_copy(p).wait_recv()
+
+        @pl.when(has_right)
+        def _():
+            home_copy(p).wait_recv()
+
+        weight = wq_ref[:, columns(b, wide)]
+        query, grad_out = queries_of(b)
+        home = rows_of(home_stats, p)
+        key_proj = key_projection(weight, jnp.concatenate([far_k[p], k_buf[b]], axis=0))
+        acc_kv[2 * rows : 3 * rows] += backward(
+            home_work,
+            p,
+            share(home, choose(rows_of(home_rest, p), rows_of(far_stats, p))),
+            [block[:, rows:] for block in key_proj],
+            project(b, query, grad_out),
+            0,
+        )
+        acc_kv[rows : 3 * rows] += backward(
+            next_work,
+            p,
+            share(rows_of(next_stats, p), rows_of(next_rest, p)),
+            key_proj,
+            project(b, by_head(next_q[p]), by_head(next_o[p])),
+            1,
+        )
+
+    chosen = index_ref[...]
+    tests = own_scores.shape[1]
+    test_at = lax.broadcasted_iota(jnp.int32, (tests, 1), 0)
+    steps = pairs + 2
+
+    def build(peer, carry):
+        hot[peer] = jnp.where(chosen == test_at + peer * tests, 1.0, 0.0).astype(BF16)
+        return carry
+
+    def step(it, carry):
+        @pl.when(it < pairs)
+        def _():
+            first(it)
+
+        lax.fori_loop(it * n_all // steps, (it + 1) * n_all // steps, build, 0)
+
+        @pl.when((it > 0) & (it <= pairs))
+        def _():
+            second(it - 1)
+
+        @pl.when(it > 1)
+        def _():
+            third(it - 2)
+
+        @pl.when(it == 1)
+        def _():
+            @pl.when(has_left)
+            def _():
+                pl.semaphore_wait(up_sem, 1)
+                x_copy(0).wait_recv()
+
+            @pl.when(has_right)
+            def _():
+                tell(up_sem, {"seq": right})
+
+            @pl.when(has_left & has_right)
+            def _():
+                x_copy(1).start()
+
+        @pl.when(it == 3)
+        def _():
+            @pl.when(has_right)
+            def _():
+                pl.semaphore_wait(down_sem, 1)
+
+            @pl.when(has_left)
+            def _():
+                tell(down_sem, {"seq": seq - 1})
+
+        return carry
+
+    lax.fori_loop(0, steps, step, 0)
+
+    @pl.when(seq > 1)
+    def _():
+        x_copy(1).wait_recv()
+
+    @pl.when(has_right)
+    def _():
+        x_copy(2).wait_recv()
+
+    acc_kv[:rows] += jnp.where(carried, acc_far[...], 0.0)
+    acc_kv[rows : 2 * rows] += jnp.where(carried, 0.0, acc_far[...])
+    projected = acc_kv[...].T + jnp.concatenate(
+        [jnp.zeros((R_OUT, 2 * rows), F32), acc_q[0], acc_q[1]], axis=1
+    )
+    inputs = x_buf[...]
+    key_pos = start - 2 * rows + lax.broadcasted_iota(jnp.int32, (1, 4 * rows), 1)
+    key_doc = doc_numbers(key_pos, ends)
+    marked = jnp.concatenate(
+        [jnp.where(key_doc == d, projected, 0.0) for d in range(DOCS)], axis=0
+    )
+    high = marked.astype(BF16)
+    rest = (marked - high.astype(F32)).astype(BF16)
+    summed = dot_nt(jnp.concatenate([high, rest], axis=0), inputs)
+    spread[...] = (summed[: DOCS * R_OUT] + summed[DOCS * R_OUT :]).reshape(spread.shape)
+    width = part.shape[2]
+    for o in range(R_OUT):
+        column = o * R_IN
+        part[column // width, :, column % width : column % width + R_IN] = spread[:, o, :].astype(BF16)
+
+    def part_copy(peer, sender, j):
+        return pltpu.make_async_remote_copy(
+            src_ref=part.at[peer],
+            dst_ref=red_in.at[sender],
+            send_sem=send1.at[j],
+            recv_sem=recv1.at[sender],
+            device_id={"seq": peer // n_head, "head": peer % n_head},
+            device_id_type=MESH,
+        )
+
+    def send_part(j, carry):
+        part_copy((red + j) % n_red, red, j).start()
+        return carry
+
+    lax.fori_loop(1, n_red, send_part, 0)
+    red_in[red] = part[red]
+
+    def take_part(j, carry):
+        part_copy((red + j) % n_red, (red + j) % n_red, j).wait_recv()
+        return carry
+
+    lax.fori_loop(1, n_red, take_part, 0)
+    red_low[...] = jnp.sum(red_in[...].astype(F32), axis=0).astype(BF16)
+
+    slot = doc * n_red + red
+
+    def slot_of(peer):
+        place = device_of(peer)
+        return place["doc"] * n_red + place["seq"] * n_head + place["head"]
+
+    def low_copy(peer, sender_slot, j):
+        return pltpu.make_async_remote_copy(
+            src_ref=red_low,
+            dst_ref=low_all.at[sender_slot],
+            send_sem=send2.at[j],
+            recv_sem=recv2.at[sender_slot],
+            device_id=device_of(peer),
+            device_id_type=MESH,
+        )
+
+    def send_low(j, carry):
+        low_copy((me + j) % n_all, slot, j).start()
+        return carry
+
+    lax.fori_loop(1, n_all, send_low, 0)
+    low_all[slot] = red_low[...]
+    local_copies[2].wait()
+
+    def take_low(j, carry):
+        low_copy((me + j) % n_all, slot_of((me + j) % n_all), j).wait_recv()
+        return carry
+
+    lax.fori_loop(1, n_all, take_low, 0)
+
+    local = jnp.zeros(own_scores.shape, F32)
+    for i in range(n_red):
+        low_ref[:, i * width : (i + 1) * width] = low_all[doc * n_red + i]
+        block = jnp.concatenate(
+            [low_all[d * n_red + i].astype(F32) for d in range(n_doc)], axis=0
+        ).astype(BF16)
+        local = local + dot_nt(block, test_buf[:, i * width : (i + 1) * width])
+    own_scores[...] = local.astype(BF16)
+
+    def score_copy(peer, sender, j):
+        return pltpu.make_async_remote_copy(
+            src_ref=own_scores,
+            dst_ref=score_all.at[sender],
+            send_sem=send3.at[j],
+            recv_sem=recv3.at[sender],
+            device_id=device_of(peer),
+            device_id_type=MESH,
+        )
+
+    def send_score(j, carry):
+        score_copy((me + j) % n_all, me, j).start()
+        return carry
+
+    lax.fori_loop(1, n_all, send_score, 0)
+    score_all[me] = local.astype(BF16)
+    def select(j, total):
+        peer = (me + j) % n_all
+
+        @pl.when(j > 0)
+        def _():
+            score_copy(peer, peer, j).wait_recv()
+
+        return total + dot(score_all[peer], hot[peer])
+
+    scores_ref[...] = lax.fori_loop(0, n_all, select, jnp.zeros(scores_ref.shape, F32))
+
+    @pl.when(has_right)
+    def _():
+        x_copy(0).wait_send()
+
+        def sent(p, carry):
+            for copy in near_copies(p) + far_copies(p) + [rest_copy(p)]:
+                copy.wait_send()
+            return carry
+
+        lax.fori_loop(0, pairs, sent, 0)
+
+    @pl.when(has_left)
+    def _():
+        x_copy(2).wait_send()
+
+        def sent_back(p, carry):
+            for copy in next_copies(p) + [home_copy(p)]:
+                copy.wait_send()
+            return carry
+
+        lax.fori_loop(0, pairs, sent_back, 0)
+
+    @pl.when(has_left & has_right)
+    def _():
+        x_copy(1).wait_send()
+
+    def sent_part(j, carry):
+        part_copy((red + j) % n_red, red, j).wait_send()
+        return carry
+
+    lax.fori_loop(1, n_red, sent_part, 0)
+
+    def sent_rest(j, carry):
+        low_copy((me + j) % n_all, slot, j).wait_send()
+        score_copy((me + j) % n_all, me, j).wait_send()
+        return carry
+
+    lax.fori_loop(1, n_all, sent_rest, 0)
+
+
 def hand_over(low_in, scores_in, low_out, scores_out):
     low_out[...] = low_in[...]
     scores_out[...] = scores_in[...]
@@ -607,10 +1272,119 @@
     tests = test_grads.shape[0]
     selected = test_index.shape[0]
     vmem = pl.BlockSpec(memory_space=pltpu.VMEM)
+    paired = longest <= min(2 * rows, WINDOW) and groups % 2 == 0
     anywhere = pl.BlockSpec(memory_space=pl.ANY)
     dma = pltpu.SemaphoreType.DMA
+    chain_scratch = [
+        pltpu.VMEM((rows + half, queries.shape[2]), BF16),
+        pltpu.VMEM((rows + half, queries.shape[2]), BF16),
+        pltpu.VMEM((groups, extent, HDIM), BF16),
+        pltpu.VMEM((groups, extent, HDIM), BF16),
+        pltpu.VMEM((R_IN, extent), BF16),
+        pltpu.VMEM(test_grads.shape, BF16),
+        pltpu.VMEM((3, half, extent - half), F32),
+        pltpu.VMEM((3, half, R_OUT), F32),
+        pltpu.VMEM((R_OUT, extent), F32),
+        pltpu.VMEM((DOCS, R_OUT, R_IN), F32),
+        pltpu.VMEM((n_red, DOCS, width), BF16),
+        pltpu.VMEM((n_red, DOCS, width), BF16),
+        pltpu.VMEM((DOCS, width), BF16),
+        pltpu.VMEM((n_all, DOCS, width), BF16),
+        pltpu.VMEM((n_doc * DOCS, tests), BF16),
+        pltpu.VMEM((n_all, n_doc * DOCS, tests), BF16),
+        pltpu.VMEM((n_all, tests, selected), BF16),
+        dma((3,)),
+        dma((2, groups)),
+        dma((hops, groups)),
+        dma((hops, groups)),
+        dma((hops, groups)),
+        dma((hops, groups)),
+        dma((hops + 1,)),
+        dma((hops + 1,)),
+        dma((4, groups)),
+        dma((4, groups)),
+        dma((n_red,)),
+        dma((n_red,)),
+        dma((n_all,)),
+        dma((n_all,)),
+        dma((n_all,)),
+        dma((n_all,)),
+        pltpu.SemaphoreType.REGULAR,
+        pltpu.SemaphoreType.REGULAR,
+    ]
+    pairs = max(groups // 2, 1)
+    stacked = queries.shape[2] // groups // HDIM * rows
+    stats = pltpu.VMEM((pairs, 8, stacked), F32)
+    shared = pltpu.VMEM((pairs, rows, HDIM), BF16)
+    pair_scratch = [
+        pltpu.VMEM((rows, queries.shape[2]), BF16),
+        pltpu.VMEM((rows, queries.shape[2]), BF16),
+        pltpu.VMEM((groups, rows, HDIM), BF16),
+        pltpu.VMEM((groups, rows, HDIM), BF16),
+        shared,
+        shared,
+        shared,
+        shared,
+        shared,
+        shared,
+        pltpu.VMEM((pairs, rows, queries.shape[2] // groups), BF16),
+        pltpu.VMEM((pairs, rows, queries.shape[2] // groups), BF16),
+        pltpu.VMEM((R_IN, 4 * rows), BF16),
+        pltpu.VMEM(test_grads.shape, BF16),
+        pltpu.VMEM((2 * rows, rows), F32),
+        pltpu.VMEM((rows, rows), F32),
+        pltpu.VMEM((2 * rows, rows), F32),
+        pltpu.VMEM((pairs, 2, 2 * rows, stacked), F32),
+        pltpu.VMEM((1, 2, rows, stacked), F32),
+        pltpu.VMEM((pairs, 2, rows, stacked), F32),
+        pltpu.VMEM((pairs, 2, 2 * rows, stacked), F32),
+        stats,
+        stats,
+        stats,
+        stats,
+        stats,
+        stats,
+        pltpu.VMEM((2, R_OUT, rows), F32),
+        pltpu.VMEM((4 * rows, R_OUT), F32),
+        pltpu.VMEM((rows, R_OUT), F32),
+        pltpu.VMEM((DOCS, R_OUT, R_IN), F32),
+        pltpu.VMEM((n_red, DOCS, width), BF16),
+        pltpu.VMEM((n_red, DOCS, width), BF16),
+        pltpu.VMEM((DOCS, width), BF16),
+        pltpu.VMEM((n_all, DOCS, width), BF16),
+        pltpu.VMEM((n_doc * DOCS, tests), BF16),
+        pltpu.VMEM((n_all, n_doc * DOCS, tests), BF16),
+        pltpu.VMEM((n_all, tests, selected), BF16),
+        dma((3,)),
+        dma((2, groups)),
+        dma((2, pairs)),
+        dma((2, pairs)),
+        dma((2, pairs)),
+        dma((2, pairs)),
+        dma((2, pairs)),
+        dma((2, pairs)),
+        dma((3,)),
+        dma((3,)),
+        dma((pairs,)),
+        dma((pairs,)),
+        dma((pairs,)),
+        dma((pairs,)),
+        dma((n_red,)),
+        dma((n_red,)),
+        dma((n_all,)),
+        dma((n_all,)),
+        dma((n_all,)),
+        dma((n_all,)),
+        pltpu.SemaphoreType.REGULAR,
+        pltpu.SemaphoreType.REGULAR,
+    ]
+    sizes = (n_seq, n_doc, n_head)
+    if paired:
+        work, scratch = functools.partial(pair_kernel, sizes), pair_scratch
+    else:
+        work, scratch = functools.partial(kernel, hops, sizes), chain_scratch
     doc_low, scores = pl.pallas_call(
-        functools.partial(kernel, hops, (n_seq, n_doc, n_head)),
+        work,
         out_shape=(
             jax.ShapeDtypeStruct((DOCS, R_OUT * R_IN), BF16),
             jax.ShapeDtypeStruct((n_doc * DOCS, selected), F32),
@@ -628,43 +1402,7 @@
             vmem,
         ],
         out_specs=(vmem, vmem),
-        scratch_shapes=[
-            pltpu.VMEM((rows + half, queries.shape[2]), BF16),
-            pltpu.VMEM((rows + half, queries.shape[2]), BF16),
-            pltpu.VMEM((groups, extent, HDIM), BF16),
-            pltpu.VMEM((groups, extent, HDIM), BF16),
-            pltpu.VMEM((R_IN, extent), BF16),
-            pltpu.VMEM(test_grads.shape, BF16),
-            pltpu.VMEM((3, half, extent - half), F32),
-            pltpu.VMEM((3, half, R_OUT), F32),
-            pltpu.VMEM((R_OUT, extent), F32),
-            pltpu.VMEM((DOCS, R_OUT, R_IN), F32),
-            pltpu.VMEM((n_red, DOCS, width), BF16),
-            pltpu.VMEM((n_red, DOCS, width), BF16),
-            pltpu.VMEM((DOCS, width), BF16),
-            pltpu.VMEM((n_all, DOCS, width), BF16),
-            pltpu.VMEM((n_doc * DOCS, tests), BF16),
-            pltpu.VMEM((n_all, n_doc * DOCS, tests), BF16),
-            pltpu.VMEM((n_all, tests, selected), BF16),
-            dma((3,)),
-            dma((2, groups)),
-            dma((hops, groups)),
-            dma((hops, groups)),
-            dma((hops, groups)),
-            dma((hops, groups)),
-            dma((hops + 1,)),
-            dma((hops + 1,)),
-            dma((4, groups)),
-            dma((4, groups)),
-            dma((n_red,)),
-            dma((n_red,)),
-            dma((n_all,)),
-            dma((n_all,)),
-            dma((n_all,)),
-            dma((n_all,)),
-            pltpu.SemaphoreType.REGULAR,
-            pltpu.SemaphoreType.REGULAR,
-        ],
+        scratch_shapes=scratch,
         compiler_params=pltpu.CompilerParams(
             collective_id=0, has_side_effects=True, vmem_limit_bytes=56 * 1024 * 1024
         ),

time: 70.9 us -> 62.9 us (0.89)
  Pallas kernels: 70.1 us -> 61.8 us
    pallas_call x1, Pallas kernels: 68.5 us -> 60.2 us  [body(): pl.pallas_call(work, out_shape=(jax.ShapeDtypeStruct((DOCS, R_OUT * R_IN)...]
where the time goes in v2:
time: 62.9 us; the launch traced here: 62.4 us
  Pallas kernels  61.8 us (98%)
  between operations  0.64 us (1%)
    pallas_call x1, Pallas kernels, body(): pl.pallas_call(work, out_shape=(jax.ShapeDtypeStruct((DOCS, R_OUT * R_IN)...  60.2 us
    pallas_call x1, Pallas kernels, body(): pl.pallas_call(hand_over, out_shape=(jax.ShapeDtypeStruct(doc_low.shape,...  1.53 us

profile of v2, /device:TPU:0, one launch (start us, length us, event | category | flops | bytes accessed | tf_op | source)
XLA Modules:
  0.0 62.4 jit_solution(9471989628818293892)
XLA Ops:
  0.6 60.2 %shard_map.113 = (bf16[8,4096]{1,0:T(8,128)(2,1)}, f32[16,1024]{1,0:T(8,128)}) custom-call(s32[1,8]{1,0:T(1,128)} %lengths.1, bf16[1,256,2048]{2,1,0:T(8,128)(2,1)} %q_hbm.1, bf16[1,256,2048]{2,1,0:T(8,128)(2,1)} %out_hbm.1, bf16[1,256,1024]{2,1,0:T(8,128)(2,1)} %k_hbm.1, bf16[1,256,1024]{2,1,0:T(8,128)(2,1)} %v_hbm.1, bf16[64,256]{1,0:T(8,128)(2,1)} %bitcast.8, ...), custom_call_target="tpu_custom_call" | custom-call | tf_op jit(solution)/shard_map/pallas_call | solution.py:1386
  60.9 1.5 %shard_map.114 = (bf16[8,4096]{1,0:T(8,128)(2,1)}, f32[16,1024]{1,0:T(8,128)}) custom-call(bf16[8,4096]{1,0:T(8,128)(2,1)} %get-tuple-element.4.low_in, f32[16,1024]{1,0:T(8,128)} %get-tuple-element.5.scores_in), custom_call_target="tpu_custom_call" | custom-call | tf_op jit(solution)/shard_map/pallas_call | solution.py:1421

commit v3 on v2

--- a/solution.py
+++ b/solution.py
@@ -584,8 +584,8 @@
     k_hbm,
     v_hbm,
     x_ref,
-    wq_ref,
-    wp_ref,
+    wq_hbm,
+    wp_hbm,
     test_hbm,
     index_ref,
     low_ref,
@@ -603,6 +603,8 @@
     next_q,
     next_o,
     x_buf,
+    wq_ref,
+    wp_ref,
     test_buf,
     bias_near,
     bias_far,
@@ -677,9 +679,21 @@
             "head": peer % n_head,
         }
 
+    def partner(mine, j, count):
+        if count & (count - 1):
+            return (mine + j) % count
+        total, bit = 0, 1
+        while bit < count:
+            ours, theirs = (mine // bit) % 2, (j // bit) % 2
+            total = total + bit * (ours + theirs - 2 * ours * theirs)
+            bit *= 2
+        return total
+
     local_copies = [
         pltpu.make_async_copy(q_hbm.at[0], q_buf, local_sem.at[0]),
         pltpu.make_async_copy(out_hbm.at[0], o_buf, local_sem.at[1]),
+        pltpu.make_async_copy(wq_hbm, wq_ref, local_sem.at[3]),
+        pltpu.make_async_copy(wp_hbm, wp_ref, local_sem.at[4]),
         pltpu.make_async_copy(test_hbm, test_buf, local_sem.at[2]),
     ]
     barrier = pltpu.get_barrier_semaphore()
@@ -837,7 +851,7 @@
     acc_q[...] = jnp.zeros_like(acc_q)
     acc_kv[...] = jnp.zeros_like(acc_kv)
     acc_far[...] = jnp.zeros_like(acc_far)
-    for copy in local_copies[:2]:
+    for copy in local_copies[:-1]:
         copy.wait()
 
     def by_head(block):
@@ -1058,18 +1072,23 @@
         def _():
             @pl.when(has_left)
             def _():
+                x_copy(0).wait_recv()
+
+            @pl.when(has_left & has_right)
+            def _():
+                x_copy(1).start()
+
+        @pl.when(it == jnp.minimum(seq, steps - 1))
+        def _():
+            @pl.when(has_left)
+            def _():
                 pl.semaphore_wait(up_sem, 1)
-                x_copy(0).wait_recv()
 
             @pl.when(has_right)
             def _():
                 tell(up_sem, {"seq": right})
 
-            @pl.when(has_left & has_right)
-            def _():
-                x_copy(1).start()
-
-        @pl.when(it == 3)
+        @pl.when(it == jnp.minimum(n_seq - right, steps - 1))
         def _():
             @pl.when(has_right)
             def _():
@@ -1157,7 +1176,7 @@
 
     lax.fori_loop(1, n_all, send_low, 0)
     low_all[slot] = red_low[...]
-    local_copies[2].wait()
+    local_copies[-1].wait()
 
     def take_low(j, carry):
         low_copy((me + j) % n_all, slot_of((me + j) % n_all), j).wait_recv()
@@ -1330,6 +1349,8 @@
         pltpu.VMEM((pairs, rows, queries.shape[2] // groups), BF16),
         pltpu.VMEM((pairs, rows, queries.shape[2] // groups), BF16),
         pltpu.VMEM((R_IN, 4 * rows), BF16),
+        pltpu.VMEM(query_projection.shape[::-1], BF16),
+        pltpu.VMEM((2, R_OUT, pair_projection.shape[1]), BF16),
         pltpu.VMEM(test_grads.shape, BF16),
         pltpu.VMEM((2 * rows, rows), F32),
         pltpu.VMEM((rows, rows), F32),
@@ -1355,7 +1376,7 @@
         pltpu.VMEM((n_doc * DOCS, tests), BF16),
         pltpu.VMEM((n_all, n_doc * DOCS, tests), BF16),
         pltpu.VMEM((n_all, tests, selected), BF16),
-        dma((3,)),
+        dma((5,)),
         dma((2, groups)),
         dma((2, pairs)),
         dma((2, pairs)),
@@ -1396,8 +1417,8 @@
             anywhere,
             anywhere,
             vmem,
-            vmem,
-            vmem,
+            anywhere if paired else vmem,
+            anywhere if paired else vmem,
             anywhere,
             vmem,
         ],

time: 62.9 us -> 59.2 us (0.941)
  Pallas kernels: 61.8 us -> 58.3 us
    pallas_call x1, Pallas kernels: 60.2 us -> 56.8 us  [body(): pl.pallas_call(work, out_shape=(jax.ShapeDtypeStruct((DOCS, R_OUT * R_IN)...]
where the time goes in v3:
time: 59.2 us; the launch traced here: 58.9 us
  Pallas kernels  58.3 us (98%)
  between operations  0.64 us (1%)
    pallas_call x1, Pallas kernels, body(): pl.pallas_call(work, out_shape=(jax.ShapeDtypeStruct((DOCS, R_OUT * R_IN)...  56.8 us
    pallas_call x1, Pallas kernels, body(): pl.pallas_call(hand_over, out_shape=(jax.ShapeDtypeStruct(doc_low.shape,...  1.53 us

profile of v3, /device:TPU:0, one launch (start us, length us, event | category | flops | bytes accessed | tf_op | source)
XLA Modules:
  0.0 58.9 jit_solution(12822377343999959004)
XLA Ops:
  0.6 56.8 %shard_map.113 = (bf16[8,4096]{1,0:T(8,128)(2,1)}, f32[16,1024]{1,0:T(8,128)}) custom-call(s32[1,8]{1,0:T(1,128)} %lengths.1, bf16[1,256,2048]{2,1,0:T(8,128)(2,1)} %q_hbm.1, bf16[1,256,2048]{2,1,0:T(8,128)(2,1)} %out_hbm.1, bf16[1,256,1024]{2,1,0:T(8,128)(2,1)} %k_hbm.1, bf16[1,256,1024]{2,1,0:T(8,128)(2,1)} %v_hbm.1, bf16[64,256]{1,0:T(8,128)(2,1)} %bitcast.8, ...), custom_call_target="tpu_custom_call" | custom-call | tf_op jit(solution)/shard_map/pallas_call | solution.py:1407
  57.4 1.5 %shard_map.114 = (bf16[8,4096]{1,0:T(8,128)(2,1)}, f32[16,1024]{1,0:T(8,128)}) custom-call(bf16[8,4096]{1,0:T(8,128)(2,1)} %get-tuple-element.4.low_in, f32[16,1024]{1,0:T(8,128)} %get-tuple-element.5.scores_in), custom_call_target="tpu_custom_call" | custom-call | tf_op jit(solution)/shard_map/pallas_call | solution.py:1442

commit v4 on v3

--- a/solution.py
+++ b/solution.py
@@ -594,14 +594,10 @@
     o_buf,
     k_buf,
     v_buf,
-    near_k,
-    near_v,
-    far_k,
-    far_v,
-    pass_k,
-    pass_v,
-    next_q,
-    next_o,
+    near,
+    far,
+    passing,
+    following,
     x_buf,
     wq_ref,
     wp_ref,
@@ -613,6 +609,9 @@
     far_work,
     home_work,
     next_work,
+    near_proj,
+    home_proj,
+    row_proj,
     near_stats,
     far_stats,
     home_stats,
@@ -631,7 +630,6 @@
     score_all,
     hot,
     local_sem,
-    own_sem,
     nsend,
     nrecv,
     fsend,
@@ -658,8 +656,8 @@
     doc = lax.axis_index("doc")
     head = lax.axis_index("head")
     rows = x_ref.shape[1]
-    groups = k_buf.shape[0]
-    pairs = near_k.shape[0]
+    groups = k_buf.shape[1] // HDIM
+    pairs = near.shape[0]
     sharing = q_buf.shape[1] // (groups * HDIM)
     wide = sharing * HDIM
     factor = 1.0 / math.sqrt(QUERY_SCALE)
@@ -679,19 +677,11 @@
             "head": peer % n_head,
         }
 
-    def partner(mine, j, count):
-        if count & (count - 1):
-            return (mine + j) % count
-        total, bit = 0, 1
-        while bit < count:
-            ours, theirs = (mine // bit) % 2, (j // bit) % 2
-            total = total + bit * (ours + theirs - 2 * ours * theirs)
-            bit *= 2
-        return total
-
     local_copies = [
         pltpu.make_async_copy(q_hbm.at[0], q_buf, local_sem.at[0]),
         pltpu.make_async_copy(out_hbm.at[0], o_buf, local_sem.at[1]),
+        pltpu.make_async_copy(k_hbm.at[0], k_buf, local_sem.at[5]),
+        pltpu.make_async_copy(v_hbm.at[0], v_buf, local_sem.at[6]),
         pltpu.make_async_copy(wq_hbm, wq_ref, local_sem.at[3]),
         pltpu.make_async_copy(wp_hbm, wp_ref, local_sem.at[4]),
         pltpu.make_async_copy(test_hbm, test_buf, local_sem.at[2]),
@@ -717,23 +707,10 @@
     def columns(g, size):
         return pl.ds(pl.multiple_of(g * size, size), size)
 
-    def own_copies(g):
-        cols = columns(g, HDIM)
-        return (
-            pltpu.make_async_copy(k_hbm.at[0, :, cols], k_buf.at[g], own_sem.at[0, g]),
-            pltpu.make_async_copy(v_hbm.at[0, :, cols], v_buf.at[g], own_sem.at[1, g]),
-        )
-
-    def start_own(g, carry):
-        for copy in own_copies(g):
-            copy.start()
-        return carry
-
-    lax.fori_loop(0, groups, start_own, 0)
     for copy in local_copies:
         copy.start()
-    near = has_left.astype(jnp.int32) + has_right.astype(jnp.int32)
-    pl.semaphore_wait(barrier, n_doc + n_head - 2 + near)
+    peers = has_left.astype(jnp.int32) + has_right.astype(jnp.int32)
+    pl.semaphore_wait(barrier, n_doc + n_head - 2 + peers)
 
     def remote(src, dst, send, recv, place):
         return pltpu.make_async_remote_copy(
@@ -748,22 +725,25 @@
     def near_copies(p):
         cols = columns(2 * p, HDIM)
         return [
-            remote(hbm.at[0, :, cols], buf.at[p], nsend.at[i, p], nrecv.at[i, p], right)
-            for i, (hbm, buf) in enumerate(((k_hbm, near_k), (v_hbm, near_v)))
+            remote(hbm.at[0, :, cols], near.at[p, i], nsend, nrecv.at[p], right)
+            for i, hbm in enumerate((k_hbm, v_hbm))
         ]
 
-    def far_copies(p):
-        return [
-            remote(src.at[p], buf.at[p], fsend.at[i, p], frecv.at[i, p], right)
-            for i, (src, buf) in enumerate(((pass_k, far_k), (pass_v, far_v)))
-        ]
+    def near_all(p):
+        return remote(near.at[p], near.at[p], nsend, nrecv.at[p], right)
+
+    def far_copy(p):
+        return remote(passing.at[p], far.at[p], fsend, frecv.at[p], right)
 
     def next_copies(p):
         many = columns(2 * p + 1, wide)
         return [
-            remote(hbm.at[0, :, many], buf.at[p], qsend.at[i, p], qrecv.at[i, p], seq - 1)
-            for i, (hbm, buf) in enumerate(((q_hbm, next_q), (out_hbm, next_o)))
+            remote(hbm.at[0, :, many], following.at[p, i], qsend, qrecv.at[p], seq - 1)
+            for i, hbm in enumerate((q_hbm, out_hbm))
         ]
+
+    def next_all(p):
+        return remote(following.at[p], following.at[p], qsend, qrecv.at[p], seq - 1)
 
     def x_copy(i):
         source = x_buf.at[:, rows : 2 * rows] if i == 1 else x_ref
@@ -772,10 +752,10 @@
         return remote(source, x_buf.at[:, at : at + rows], xsend.at[i], xrecv.at[i], place)
 
     def home_copy(p):
-        return remote(home_stats.at[p], next_rest.at[p], hsend.at[p], hrecv.at[p], seq - 1)
+        return remote(home_stats.at[p], next_rest.at[p], hsend, hrecv.at[p], seq - 1)
 
     def rest_copy(p):
-        return remote(next_stats.at[p], home_rest.at[p], tsend.at[p], trecv.at[p], right)
+        return remote(next_stats.at[p], home_rest.at[p], tsend, trecv.at[p], right)
 
     def start_pair(p):
         @pl.when(has_right)
@@ -804,7 +784,7 @@
     @pl.when(seq == 0)
     def _():
         x_buf[:, rows : 2 * rows] = jnp.zeros((R_IN, rows), BF16)
-        for buf in (near_k, near_v, far_k, far_v, home_rest):
+        for buf in (near, far, home_rest):
             buf[...] = jnp.zeros(buf.shape, buf.dtype)
 
     @pl.when(seq < 2)
@@ -814,8 +794,7 @@
     @pl.when(right == n_seq)
     def _():
         x_buf[:, 3 * rows :] = jnp.zeros((R_IN, rows), BF16)
-        for buf in (next_q, next_o):
-            buf[...] = jnp.zeros(buf.shape, buf.dtype)
+        following[...] = jnp.zeros(following.shape, BF16)
         next_rest[...] = jnp.ones(next_rest.shape, F32)
 
     ends = []
@@ -911,63 +890,67 @@
         many = columns(g, wide)
         return by_head(q_buf[:, many]), by_head(o_buf[:, many])
 
+    def own_keys(g):
+        cols = columns(g, HDIM)
+        return k_buf[:, cols], v_buf[:, cols]
+
     def first(p):
         a, b = 2 * p, 2 * p + 1
-        for g in (a, b):
-            for copy in own_copies(g):
-                copy.wait()
+        keys_a, values_a = own_keys(a)
+        keys_b, values_b = own_keys(b)
 
         @pl.when(has_left)
         def _():
-            for copy in near_copies(p):
-                copy.wait_recv()
-
-        pass_k[p] = jnp.where(covered, near_k[p], k_buf[b])
-        pass_v[p] = jnp.where(covered, near_v[p], v_buf[b])
+            near_all(p).wait_recv()
+
+        passing[p, 0] = jnp.where(covered, near[p, 0], keys_b)
+        passing[p, 1] = jnp.where(covered, near[p, 1], values_b)
 
         @pl.when(has_right)
         def _():
-            for copy in far_copies(p):
-                copy.start()
+            far_copy(p).start()
 
         @pl.when(p + 2 < pairs)
         def _():
             start_pair(p + 2)
 
         query, grad_out = queries_of(b)
-        forward(
-            k_buf[b], v_buf[b], query, grad_out, bias_near[rows:], home_work, p, home_stats, p
-        )
+        forward(keys_b, values_b, query, grad_out, bias_near[rows:], home_work, p, home_stats, p)
 
         @pl.when(has_left)
         def _():
             home_copy(p).start()
 
+        weight = wq_ref[:, columns(b, wide)]
+        for h, block in enumerate(key_projection(weight, keys_b)):
+            home_proj[p, h] = block
+        row_proj[p, 2], row_proj[p, 3] = project(b, query, grad_out)
         query, grad_out = queries_of(a)
-        keys = jnp.concatenate([near_k[p], k_buf[a]], axis=0)
-        values = jnp.concatenate([near_v[p], v_buf[a]], axis=0)
+        keys = jnp.concatenate([near[p, 0], keys_a], axis=0)
+        values = jnp.concatenate([near[p, 1], values_a], axis=0)
         forward(keys, values, query, grad_out, bias_near[...], near_work, p, near_stats, p)
+        weight = wq_ref[:, columns(a, wide)]
+        for h, block in enumerate(key_projection(weight, keys)):
+            near_proj[p, h] = block
+        row_proj[p, 0], row_proj[p, 1] = project(a, query, grad_out)
 
     def second(p):
         a, b = 2 * p, 2 * p + 1
 
         @pl.when(has_left)
         def _():
-            for copy in far_copies(p):
-                copy.wait_recv()
+            far_copy(p).wait_recv()
 
         @pl.when(has_right)
         def _():
-            for copy in next_copies(p):
-                copy.wait_recv()
-
-        keys = jnp.concatenate([far_k[p], k_buf[b]], axis=0)
-        values = jnp.concatenate([far_v[p], v_buf[b]], axis=0)
+            next_all(p).wait_recv()
+
+        keys_b, values_b = own_keys(b)
         forward(
-            keys,
-            values,
-            by_head(next_q[p]),
-            by_head(next_o[p]),
+            jnp.concatenate([far[p, 0], keys_b], axis=0),
+            jnp.concatenate([far[p, 1], values_b], axis=0),
+            by_head(following[p, 0]),
+            by_head(following[p, 1]),
             bias_next[...],
             next_work,
             p,
@@ -979,41 +962,40 @@
         def _():
             rest_copy(p).start()
 
-        query_a, out_a = queries_of(a)
-        query_b, out_b = queries_of(b)
-        query = jnp.where(carried, query_a, query_b)
-        grad_out = jnp.where(carried, out_a, out_b)
+        many_a, many_b = columns(a, wide), columns(b, wide)
+        query = by_head(jnp.where(carried, q_buf[:, many_a], q_buf[:, many_b]))
+        grad_out = by_head(jnp.where(carried, o_buf[:, many_a], o_buf[:, many_b]))
         forward(
-            far_k[p], far_v[p], query, grad_out, bias_far[...], far_work, 0, far_stats, p
+            far[p, 0], far[p, 1], query, grad_out, bias_far[...], far_work, 0, far_stats, p
         )
         mine = rows_of(near_stats, p)
         home = rows_of(home_stats, p)
-        far = rows_of(far_stats, p)
-        none = (jnp.full_like(far[0], 2 * NEG_FILL), jnp.zeros_like(far[1]), jnp.zeros_like(far[2]))
-        weight_a, weight_b = wq_ref[:, columns(a, wide)], wq_ref[:, columns(b, wide)]
-        weight = jnp.where(carried, weight_a, weight_b)
-        project_a = project(a, query_a, out_a)
-        keys = jnp.concatenate([near_k[p], k_buf[a]], axis=0)
+        far_rows = rows_of(far_stats, p)
+        none = (jnp.full_like(mine[0], 2 * NEG_FILL), jnp.zeros_like(mine[1]), jnp.zeros_like(mine[2]))
         acc_kv[rows : 3 * rows] += backward(
             near_work,
             p,
-            share(mine, choose(far, none)),
-            key_projection(weight_a, keys),
-            project_a,
+            share(mine, choose(far_rows, none)),
+            [near_proj[p, h] for h in range(sharing)],
+            (row_proj[p, 0], row_proj[p, 1]),
             0,
         )
-        project_b = project(b, query_b, out_b)
+        weight = jnp.where(carried, wq_ref[:, many_a], wq_ref[:, many_b])
+        far_proj = key_projection(weight, far[p, 0])
         acc_far[...] += backward(
             far_work,
             0,
-            share(far, choose(mine, home)),
-            key_projection(weight, far_k[p]),
-            choose(project_a, project_b),
+            share(far_rows, choose(mine, home)),
+            far_proj,
+            choose((row_proj[p, 0], row_proj[p, 1]), (row_proj[p, 2], row_proj[p, 3])),
             0,
         )
+        for h, block in enumerate(far_proj):
+            near_proj[p, h, :, :rows] = block
 
     def third(p):
         b = 2 * p + 1
+        projected = project(b, by_head(following[p, 0]), by_head(following[p, 1]))
 
         @pl.when(has_left)
         def _():
@@ -1023,24 +1005,26 @@
         def _():
             home_copy(p).wait_recv()
 
-        weight = wq_ref[:, columns(b, wide)]
-        query, grad_out = queries_of(b)
         home = rows_of(home_stats, p)
-        key_proj = key_projection(weight, jnp.concatenate([far_k[p], k_buf[b]], axis=0))
+        home_keys = [home_proj[p, h] for h in range(sharing)]
         acc_kv[2 * rows : 3 * rows] += backward(
             home_work,
             p,
             share(home, choose(rows_of(home_rest, p), rows_of(far_stats, p))),
-            [block[:, rows:] for block in key_proj],
-            project(b, query, grad_out),
+            home_keys,
+            (row_proj[p, 2], row_proj[p, 3]),
             0,
         )
+        key_proj = [
+            jnp.concatenate([near_proj[p, h, :, :rows], home_keys[h]], axis=1)
+            for h in range(sharing)
+        ]
         acc_kv[rows : 3 * rows] += backward(
             next_work,
             p,
             share(rows_of(next_stats, p), rows_of(next_rest, p)),
             key_proj,
-            project(b, by_head(next_q[p]), by_head(next_o[p])),
+            projected,
             1,
         )
 
@@ -1057,8 +1041,7 @@
         @pl.when(it < pairs)
         def _():
             first(it)
-
-        lax.fori_loop(it * n_all // steps, (it + 1) * n_all // steps, build, 0)
+            lax.fori_loop(it * n_all // pairs, (it + 1) * n_all // pairs, build, 0)
 
         @pl.when((it > 0) & (it <= pairs))
         def _():
@@ -1121,68 +1104,48 @@
     marked = jnp.concatenate(
         [jnp.where(key_doc == d, projected, 0.0) for d in range(DOCS)], axis=0
     )
-    high = marked.astype(BF16)
-    rest = (marked - high.astype(F32)).astype(BF16)
-    summed = dot_nt(jnp.concatenate([high, rest], axis=0), inputs)
-    spread[...] = (summed[: DOCS * R_OUT] + summed[DOCS * R_OUT :]).reshape(spread.shape)
+    spread[...] = dot_nt(marked.astype(BF16), inputs).reshape(spread.shape)
     width = part.shape[2]
     for o in range(R_OUT):
         column = o * R_IN
         part[column // width, :, column % width : column % width + R_IN] = spread[:, o, :].astype(BF16)
 
-    def part_copy(peer, sender, j):
+    def block_copy(src, dst, send, recv, place):
         return pltpu.make_async_remote_copy(
-            src_ref=part.at[peer],
-            dst_ref=red_in.at[sender],
-            send_sem=send1.at[j],
-            recv_sem=recv1.at[sender],
-            device_id={"seq": peer // n_head, "head": peer % n_head},
+            src_ref=src,
+            dst_ref=dst,
+            send_sem=send,
+            recv_sem=recv,
+            device_id=place,
             device_id_type=MESH,
         )
 
     def send_part(j, carry):
-        part_copy((red + j) % n_red, red, j).start()
+        peer = (red + j) % n_red
+        place = {"seq": peer // n_head, "head": peer % n_head}
+        block_copy(part.at[peer], red_in.at[red], send1, recv1, place).start()
         return carry
 
     lax.fori_loop(1, n_red, send_part, 0)
     red_in[red] = part[red]
-
-    def take_part(j, carry):
-        part_copy((red + j) % n_red, (red + j) % n_red, j).wait_recv()
-        return carry
-
-    lax.fori_loop(1, n_red, take_part, 0)
+    others = red_in.at[pl.ds(0, n_red - 1)]
+    parts = block_copy(others, others, send1, recv1, device_of(me))
+    parts.wait_recv()
     red_low[...] = jnp.sum(red_in[...].astype(F32), axis=0).astype(BF16)
 
     slot = doc * n_red + red
 
-    def slot_of(peer):
-        place = device_of(peer)
-        return place["doc"] * n_red + place["seq"] * n_head + place["head"]
-
-    def low_copy(peer, sender_slot, j):
-        return pltpu.make_async_remote_copy(
-            src_ref=red_low,
-            dst_ref=low_all.at[sender_slot],
-            send_sem=send2.at[j],
-            recv_sem=recv2.at[sender_slot],
-            device_id=device_of(peer),
-            device_id_type=MESH,
-        )
-
     def send_low(j, carry):
-        low_copy((me + j) % n_all, slot, j).start()
+        place = device_of((me + j) % n_all)
+        block_copy(red_low, low_all.at[slot], send2, recv2, place).start()
         return carry
 
     lax.fori_loop(1, n_all, send_low, 0)
     low_all[slot] = red_low[...]
     local_copies[-1].wait()
-
-    def take_low(j, carry):
-        low_copy((me + j) % n_all, slot_of((me + j) % n_all), j).wait_recv()
-        return carry
-
-    lax.fori_loop(1, n_all, take_low, 0)
+    others = low_all.at[pl.ds(0, n_all - 1)]
+    lows = block_copy(others, others, send2, recv2, device_of(me))
+    lows.wait_recv()
 
     local = jnp.zeros(own_scores.shape, F32)
     for i in range(n_red):
@@ -1193,28 +1156,24 @@
         local = local + dot_nt(block, test_buf[:, i * width : (i + 1) * width])
     own_scores[...] = local.astype(BF16)
 
-    def score_copy(peer, sender, j):
-        return pltpu.make_async_remote_copy(
-            src_ref=own_scores,
-            dst_ref=score_all.at[sender],
-            send_sem=send3.at[j],
-            recv_sem=recv3.at[sender],
-            device_id=device_of(peer),
-            device_id_type=MESH,
+    def score_copy(peer, sender):
+        return block_copy(
+            own_scores, score_all.at[sender], send3, recv3.at[sender], device_of(peer)
         )
 
     def send_score(j, carry):
-        score_copy((me + j) % n_all, me, j).start()
+        score_copy((me + j) % n_all, me).start()
         return carry
 
     lax.fori_loop(1, n_all, send_score, 0)
     score_all[me] = local.astype(BF16)
+
     def select(j, total):
         peer = (me + j) % n_all
 
         @pl.when(j > 0)
         def _():
-            score_copy(peer, peer, j).wait_recv()
+            score_copy(peer, peer).wait_recv()
 
         return total + dot(score_all[peer], hot[peer])
 
@@ -1223,41 +1182,24 @@
     @pl.when(has_right)
     def _():
         x_copy(0).wait_send()
-
-        def sent(p, carry):
-            for copy in near_copies(p) + far_copies(p) + [rest_copy(p)]:
-                copy.wait_send()
-            return carry
-
-        lax.fori_loop(0, pairs, sent, 0)
+        remote(near, near, nsend, nrecv.at[0], right).wait_send()
+        remote(far, far, fsend, frecv.at[0], right).wait_send()
+        remote(next_stats, next_stats, tsend, trecv.at[0], right).wait_send()
 
     @pl.when(has_left)
     def _():
         x_copy(2).wait_send()
-
-        def sent_back(p, carry):
-            for copy in next_copies(p) + [home_copy(p)]:
-                copy.wait_send()
-            return carry
-
-        lax.fori_loop(0, pairs, sent_back, 0)
+        remote(following, following, qsend, qrecv.at[0], seq - 1).wait_send()
+        remote(home_stats, home_stats, hsend, hrecv.at[0], seq - 1).wait_send()
 
     @pl.when(has_left & has_right)
     def _():
         x_copy(1).wait_send()
 
-    def sent_part(j, carry):
-        part_copy((red + j) % n_red, red, j).wait_send()
-        return carry
-
-    lax.fori_loop(1, n_red, sent_part, 0)
-
-    def sent_rest(j, carry):
-        low_copy((me + j) % n_all, slot, j).wait_send()
-        score_copy((me + j) % n_all, me, j).wait_send()
-        return carry
-
-    lax.fori_loop(1, n_all, sent_rest, 0)
+    parts.wait_send()
+    lows.wait_send()
+    others = score_all.at[pl.ds(0, n_all - 1)]
+    block_copy(others, others, send3, recv3.at[0], device_of(me)).wait_send()
 
 
 def hand_over(low_in, scores_in, low_out, scores_out):
@@ -1334,20 +1276,17 @@
     pairs = max(groups // 2, 1)
     stacked = queries.shape[2] // groups // HDIM * rows
     stats = pltpu.VMEM((pairs, 8, stacked), F32)
-    shared = pltpu.VMEM((pairs, rows, HDIM), BF16)
+    shared = pltpu.VMEM((pairs, 2, rows, HDIM), BF16)
+    span = queries.shape[2] // groups
     pair_scratch = [
         pltpu.VMEM((rows, queries.shape[2]), BF16),
         pltpu.VMEM((rows, queries.shape[2]), BF16),
-        pltpu.VMEM((groups, rows, HDIM), BF16),
-        pltpu.VMEM((groups, rows, HDIM), BF16),
+        pltpu.VMEM((rows, keys.shape[2]), BF16),
+        pltpu.VMEM((rows, keys.shape[2]), BF16),
         shared,
         shared,
         shared,
-        shared,
-        shared,
-        shared,
-        pltpu.VMEM((pairs, rows, queries.shape[2] // groups), BF16),
-        pltpu.VMEM((pairs, rows, queries.shape[2] // groups), BF16),
+        pltpu.VMEM((pairs, 2, rows, span), BF16),
         pltpu.VMEM((R_IN, 4 * rows), BF16),
         pltpu.VMEM(query_projection.shape[::-1], BF16),
         pltpu.VMEM((2, R_OUT, pair_projection.shape[1]), BF16),
@@ -1359,6 +1298,9 @@
         pltpu.VMEM((1, 2, rows, stacked), F32),
         pltpu.VMEM((pairs, 2, rows, stacked), F32),
         pltpu.VMEM((pairs, 2, 2 * rows, stacked), F32),
+        pltpu.VMEM((pairs, span // HDIM, R_OUT, 2 * rows), BF16),
+        pltpu.VMEM((pairs, span // HDIM, R_OUT, rows), BF16),
+        pltpu.VMEM((pairs, 4, R_OUT, stacked), BF16),
         stats,
         stats,
         stats,
@@ -1376,25 +1318,24 @@
         pltpu.VMEM((n_doc * DOCS, tests), BF16),
         pltpu.VMEM((n_all, n_doc * DOCS, tests), BF16),
         pltpu.VMEM((n_all, tests, selected), BF16),
-        dma((5,)),
-        dma((2, groups)),
-        dma((2, pairs)),
-        dma((2, pairs)),
-        dma((2, pairs)),
-        dma((2, pairs)),
-        dma((2, pairs)),
-        dma((2, pairs)),
+        dma((7,)),
+        dma(()),
+        dma((pairs,)),
+        dma(()),
+        dma((pairs,)),
+        dma(()),
+        dma((pairs,)),
         dma((3,)),
         dma((3,)),
+        dma(()),
         dma((pairs,)),
+        dma(()),
         dma((pairs,)),
-        dma((pairs,)),
-        dma((pairs,)),
-        dma((n_red,)),
-        dma((n_red,)),
-        dma((n_all,)),
-        dma((n_all,)),
-        dma((n_all,)),
+        dma(()),
+        dma(()),
+        dma(()),
+        dma(()),
+        dma(()),
         dma((n_all,)),
         pltpu.SemaphoreType.REGULAR,
         pltpu.SemaphoreType.REGULAR,

time: 59.2 us -> 55.7 us (0.941)
  Pallas kernels: 58.3 us -> 54.8 us
    pallas_call x1, Pallas kernels: 56.8 us -> 53.3 us  [body(): pl.pallas_call(work, out_shape=(jax.ShapeDtypeStruct((DOCS, R_OUT * R_IN)...]
where the time goes in v4:
time: 55.7 us; the launch traced here: 55.5 us
  Pallas kernels  54.8 us (98%)
  between operations  0.64 us (1%)
    pallas_call x1, Pallas kernels, body(): pl.pallas_call(work, out_shape=(jax.ShapeDtypeStruct((DOCS, R_OUT * R_IN)...  53.3 us
    pallas_call x1, Pallas kernels, body(): pl.pallas_call(hand_over, out_shape=(jax.ShapeDtypeStruct(doc_low.shape,...  1.53 us

profile of v4, /device:TPU:0, one launch (start us, length us, event | category | flops | bytes accessed | tf_op | source)
XLA Modules:
  0.0 55.5 jit_solution(18166965084742142710)
XLA Ops:
  0.6 53.3 %shard_map.113 = (bf16[8,4096]{1,0:T(8,128)(2,1)}, f32[16,1024]{1,0:T(8,128)}) custom-call(s32[1,8]{1,0:T(1,128)} %lengths.1, bf16[1,256,2048]{2,1,0:T(8,128)(2,1)} %q_hbm.1, bf16[1,256,2048]{2,1,0:T(8,128)(2,1)} %out_hbm.1, bf16[1,256,1024]{2,1,0:T(8,128)(2,1)} %k_hbm.1, bf16[1,256,1024]{2,1,0:T(8,128)(2,1)} %v_hbm.1, bf16[64,256]{1,0:T(8,128)(2,1)} %bitcast.8, ...), custom_call_target="tpu_custom_call" | custom-call | tf_op jit(solution)/shard_map/pallas_call | solution.py:1348
  53.9 1.5 %shard_map.114 = (bf16[8,4096]{1,0:T(8,128)(2,1)}, f32[16,1024]{1,0:T(8,128)}) custom-call(bf16[8,4096]{1,0:T(8,128)(2,1)} %get-tuple-element.4.low_in, f32[16,1024]{1,0:T(8,128)} %get-tuple-element.5.scores_in), custom_call_target="tpu_custom_call" | custom-call | tf_op jit(solution)/shard_map/pallas_call | solution.py:1383

commit v5 on v4

--- a/solution.py
+++ b/solution.py
@@ -578,18 +578,18 @@
 
 def pair_kernel(
     sizes,
-    lengths,
+    lengths_hbm,
     q_hbm,
     out_hbm,
     k_hbm,
     v_hbm,
-    x_ref,
+    x_hbm,
     wq_hbm,
     wp_hbm,
     test_hbm,
-    index_ref,
-    low_ref,
-    scores_ref,
+    index_hbm,
+    low_out,
+    scores_out,
     q_buf,
     o_buf,
     k_buf,
@@ -599,6 +599,10 @@
     passing,
     following,
     x_buf,
+    lengths,
+    index_ref,
+    low_ref,
+    scores_ref,
     wq_ref,
     wp_ref,
     test_buf,
@@ -655,7 +659,7 @@
     seq = lax.axis_index("seq")
     doc = lax.axis_index("doc")
     head = lax.axis_index("head")
-    rows = x_ref.shape[1]
+    rows = q_buf.shape[0]
     groups = k_buf.shape[1] // HDIM
     pairs = near.shape[0]
     sharing = q_buf.shape[1] // (groups * HDIM)
@@ -677,6 +681,17 @@
             "head": peer % n_head,
         }
 
+    early_copies = [
+        pltpu.make_async_copy(lengths_hbm, lengths, local_sem.at[7]),
+        pltpu.make_async_copy(index_hbm, index_ref, local_sem.at[8]),
+        pltpu.make_async_copy(
+            x_hbm, x_buf.at[:, pl.ds(2 * rows, rows)], local_sem.at[9]
+        ),
+    ]
+    out_copies = [
+        pltpu.make_async_copy(low_ref, low_out, local_sem.at[7]),
+        pltpu.make_async_copy(scores_ref, scores_out, local_sem.at[8]),
+    ]
     local_copies = [
         pltpu.make_async_copy(q_hbm.at[0], q_buf, local_sem.at[0]),
         pltpu.make_async_copy(out_hbm.at[0], o_buf, local_sem.at[1]),
@@ -707,7 +722,7 @@
     def columns(g, size):
         return pl.ds(pl.multiple_of(g * size, size), size)
 
-    for copy in local_copies:
+    for copy in early_copies + local_copies:
         copy.start()
     peers = has_left.astype(jnp.int32) + has_right.astype(jnp.int32)
     pl.semaphore_wait(barrier, n_doc + n_head - 2 + peers)
@@ -746,7 +761,7 @@
         return remote(following.at[p], following.at[p], qsend, qrecv.at[p], seq - 1)
 
     def x_copy(i):
-        source = x_buf.at[:, rows : 2 * rows] if i == 1 else x_ref
+        source = x_buf.at[:, rows : 2 * rows] if i == 1 else x_hbm
         at = (rows, 0, 3 * rows)[i]
         place = seq - 1 if i == 2 else right
         return remote(source, x_buf.at[:, at : at + rows], xsend.at[i], xrecv.at[i], place)
@@ -779,8 +794,6 @@
     def _():
         x_copy(2).start()
 
-    x_buf[:, 2 * rows : 3 * rows] = x_ref[...]
-
     @pl.when(seq == 0)
     def _():
         x_buf[:, rows : 2 * rows] = jnp.zeros((R_IN, rows), BF16)
@@ -797,6 +810,8 @@
         following[...] = jnp.zeros(following.shape, BF16)
         next_rest[...] = jnp.ones(next_rest.shape, F32)
 
+    for copy in early_copies:
+        copy.wait()
     ends = []
     for k in range(DOCS):
         ends.append(lengths[0, k] + (ends[-1] if ends else 0))
@@ -1154,30 +1169,40 @@
             [low_all[d * n_red + i].astype(F32) for d in range(n_doc)], axis=0
         ).astype(BF16)
         local = local + dot_nt(block, test_buf[:, i * width : (i + 1) * width])
+    out_copies[0].start()
     own_scores[...] = local.astype(BF16)
 
-    def score_copy(peer, sender):
+    plane = n_doc * n_head
+
+    def score_copy(peer):
         return block_copy(
-            own_scores, score_all.at[sender], send3, recv3.at[sender], device_of(peer)
+            own_scores, score_all.at[me], send3, recv3.at[seq], device_of(peer)
         )
 
     def send_score(j, carry):
-        score_copy((me + j) % n_all, me).start()
+        score_copy((me + j) % n_all).start()
         return carry
 
     lax.fori_loop(1, n_all, send_score, 0)
     score_all[me] = local.astype(BF16)
 
-    def select(j, total):
-        peer = (me + j) % n_all
-
-        @pl.when(j > 0)
-        def _():
-            score_copy(peer, peer).wait_recv()
-
-        return total + dot(score_all[peer], hot[peer])
-
-    scores_ref[...] = lax.fori_loop(0, n_all, select, jnp.zeros(scores_ref.shape, F32))
+    def select(place):
+        several = jnp.concatenate(
+            [score_all[place * plane + i].astype(F32) for i in range(plane)], axis=1
+        ).astype(BF16)
+        return dot(several, hot[pl.ds(place * plane, plane)].reshape(plane * tests, -1))
+
+    if plane > 1:
+        others = score_all.at[pl.ds(0, plane - 1)]
+        block_copy(others, others, send3, recv3.at[seq], device_of(me)).wait_recv()
+    total = select(seq)
+    others = score_all.at[pl.ds(0, plane)]
+    for i in range(1, n_seq):
+        place = (seq + i) % n_seq
+        block_copy(others, others, send3, recv3.at[place], device_of(me)).wait_recv()
+        total = total + select(place)
+    scores_ref[...] = total
+    out_copies[1].start()
 
     @pl.when(has_right)
     def _():
@@ -1200,11 +1225,26 @@
     lows.wait_send()
     others = score_all.at[pl.ds(0, n_all - 1)]
     block_copy(others, others, send3, recv3.at[0], device_of(me)).wait_send()
-
-
-def hand_over(low_in, scores_in, low_out, scores_out):
-    low_out[...] = low_in[...]
-    scores_out[...] = scores_in[...]
+    for copy in out_copies:
+        copy.wait()
+
+
+def hand_over(low_in, scores_in, low_out, scores_out, low, scores, sems):
+    inward = [
+        pltpu.make_async_copy(low_in, low, sems.at[0]),
+        pltpu.make_async_copy(scores_in, scores, sems.at[1]),
+    ]
+    outward = [
+        pltpu.make_async_copy(low, low_out, sems.at[0]),
+        pltpu.make_async_copy(scores, scores_out, sems.at[1]),
+    ]
+    for copy in inward:
+        copy.start()
+    for i in range(2):
+        inward[i].wait()
+        outward[i].start()
+    for copy in outward:
+        copy.wait()
 
 
 def body(
@@ -1288,6 +1328,10 @@
         shared,
         pltpu.VMEM((pairs, 2, rows, span), BF16),
         pltpu.VMEM((R_IN, 4 * rows), BF16),
+        pltpu.SMEM(lengths.shape, jnp.int32),
+        pltpu.VMEM((1, selected), jnp.int32),
+        pltpu.VMEM((DOCS, R_OUT * R_IN), BF16),
+        pltpu.VMEM((n_doc * DOCS, selected), F32),
         pltpu.VMEM(query_projection.shape[::-1], BF16),
         pltpu.VMEM((2, R_OUT, pair_projection.shape[1]), BF16),
         pltpu.VMEM(test_grads.shape, BF16),
@@ -1318,7 +1362,7 @@
         pltpu.VMEM((n_doc * DOCS, tests), BF16),
         pltpu.VMEM((n_all, n_doc * DOCS, tests), BF16),
         pltpu.VMEM((n_all, tests, selected), BF16),
-        dma((7,)),
+        dma((10,)),
         dma(()),
         dma((pairs,)),
         dma(()),
@@ -1336,7 +1380,7 @@
         dma(()),
         dma(()),
         dma(()),
-        dma((n_all,)),
+        dma((n_seq,)),
         pltpu.SemaphoreType.REGULAR,
         pltpu.SemaphoreType.REGULAR,
     ]
@@ -1345,6 +1389,7 @@
         work, scratch = functools.partial(pair_kernel, sizes), pair_scratch
     else:
         work, scratch = functools.partial(kernel, hops, sizes), chain_scratch
+    place = anywhere if paired else vmem
     doc_low, scores = pl.pallas_call(
         work,
         out_shape=(
@@ -1352,18 +1397,18 @@
             jax.ShapeDtypeStruct((n_doc * DOCS, selected), F32),
         ),
         in_specs=[
-            pl.BlockSpec(memory_space=pltpu.SMEM),
+            anywhere if paired else pl.BlockSpec(memory_space=pltpu.SMEM),
             anywhere,
             anywhere,
             anywhere,
             anywhere,
-            vmem,
-            anywhere if paired else vmem,
-            anywhere if paired else vmem,
+            place,
+            place,
+            place,
             anywhere,
-            vmem,
+            place,
         ],
-        out_specs=(vmem, vmem),
+        out_specs=(place, place),
         scratch_shapes=scratch,
         compiler_params=pltpu.CompilerParams(
             collective_id=0, has_side_effects=True, vmem_limit_bytes=56 * 1024 * 1024
@@ -1386,8 +1431,13 @@
             jax.ShapeDtypeStruct(doc_low.shape, BF16),
             jax.ShapeDtypeStruct(scores.shape, F32),
         ),
-        in_specs=[vmem, vmem],
-        out_specs=(vmem, vmem),
+        in_specs=[anywhere, anywhere],
+        out_specs=(anywhere, anywhere),
+        scratch_shapes=[
+            pltpu.VMEM(doc_low.shape, BF16),
+            pltpu.VMEM(scores.shape, F32),
+            dma((2,)),
+        ],
     )(doc_low, scores)
 
 

time: 55.7 us -> 54.9 us (0.986)
  Pallas kernels: 54.8 us -> 54.1 us
    pallas_call x1, Pallas kernels: 53.3 us -> 52.6 us  [body(): pl.pallas_call(work, out_shape=(jax.ShapeDtypeStruct((DOCS, R_OUT * R_IN)...]
where the time goes in v5:
time: 54.9 us; the launch traced here: 54.7 us
  Pallas kernels  54.1 us (99%)
  between operations  0.64 us (1%)
    pallas_call x1, Pallas kernels, body(): pl.pallas_call(work, out_shape=(jax.ShapeDtypeStruct((DOCS, R_OUT * R_IN)...  52.6 us
    pallas_call x1, Pallas kernels, body(): pl.pallas_call(hand_over, out_shape=(jax.ShapeDtypeStruct(doc_low.shape,...  1.52 us

profile of v5, /device:TPU:0, one launch (start us, length us, event | category | flops | bytes accessed | tf_op | source)
XLA Modules:
  0.0 54.7 jit_solution(2517934449096623604)
XLA Ops:
  0.6 52.6 %shard_map.113 = (bf16[8,4096]{1,0:T(8,128)(2,1)}, f32[16,1024]{1,0:T(8,128)}) custom-call(s32[1,8]{1,0:T(1,128)} %lengths_hbm.1, bf16[1,256,2048]{2,1,0:T(8,128)(2,1)} %q_hbm.1, bf16[1,256,2048]{2,1,0:T(8,128)(2,1)} %out_hbm.1, bf16[1,256,1024]{2,1,0:T(8,128)(2,1)} %k_hbm.1, bf16[1,256,1024]{2,1,0:T(8,128)(2,1)} %v_hbm.1, bf16[64,256]{1,0:T(8,128)(2,1)} %bitcast.8, ...), custom_call_target="tpu_custom_call" | custom-call | tf_op jit(solution)/shard_map/pallas_call | solution.py:1393
  53.2 1.5 %shard_map.114 = (bf16[8,4096]{1,0:T(8,128)(2,1)}, f32[16,1024]{1,0:T(8,128)}) custom-call(bf16[8,4096]{1,0:T(8,128)(2,1)} %get-tuple-element.4.low_in, f32[16,1024]{1,0:T(8,128)} %get-tuple-element.5.scores_in), custom_call_target="tpu_custom_call" | custom-call | tf_op jit(solution)/shard_map/pallas_call | solution.py:1428

commit v6 on v5

--- a/solution.py
+++ b/solution.py
@@ -616,6 +616,11 @@
     near_proj,
     home_proj,
     row_proj,
+    home_cross,
+    next_cross,
+    next_proj,
+    grad_rest,
+    crossing,
     near_stats,
     far_stats,
     home_stats,
@@ -845,6 +850,11 @@
     acc_q[...] = jnp.zeros_like(acc_q)
     acc_kv[...] = jnp.zeros_like(acc_kv)
     acc_far[...] = jnp.zeros_like(acc_far)
+    grad_rest[...] = jnp.zeros_like(grad_rest)
+    row_doc = doc_numbers(start + lax.broadcasted_iota(jnp.int32, (1, rows), 1), ends)
+    held = jnp.where(row_doc == doc_at(start - 1), 1.0, 0.0)
+    held = jnp.concatenate([jnp.where(carried, held, 0.0)] * sharing, axis=1)
+    crossing[...] = jnp.broadcast_to(held, crossing.shape)
     for copy in local_copies[:-1]:
         copy.wait()
 
@@ -879,10 +889,13 @@
 
     def project(group, query, grad_out):
         cols = columns(group, HDIM)
-        return (
-            (dot_nt(wp_ref[0, :, cols], query) * factor).astype(BF16),
-            dot_nt(wp_ref[1, :, cols], grad_out).astype(BF16),
-        )
+        return jnp.concatenate(
+            [
+                dot_nt(wp_ref[0, :, cols], query) * factor,
+                dot_nt(wp_ref[1, :, cols], grad_out),
+            ],
+            axis=1,
+        ).astype(BF16)
 
     def key_projection(weight, keys):
         return [
@@ -894,12 +907,44 @@
         scale, centre = shares
         attention = work[at, 0] * scale
         score_grad = (attention * (work[at, 1] - centre)).astype(BF16)
-        attention_low = attention.astype(BF16)
-        crossed = dot(key_proj[0], score_grad[:, :rows])
+        stacked = jnp.concatenate(
+            [score_grad[:, h * rows : (h + 1) * rows] for h in range(sharing)], axis=0
+        )
+        acc_q[query_at] += dot(jnp.concatenate(key_proj, axis=1), stacked)
+        both = jnp.concatenate([score_grad, attention.astype(BF16)], axis=1)
+        return dot_nt(projected, both)
+
+    def prepare(work, at, shares, key_proj, x_at, cross, p):
+        size = key_proj[0].shape[1]
+        scale, centre = shares
+        attention = work[at, 0] * scale
+        score_grad = (attention * (work[at, 1] - centre)).astype(BF16)
+        attention = attention.astype(BF16)
+        inputs = x_buf[:, x_at : x_at + size]
+        for h in range(sharing):
+            cols = slice(h * rows, (h + 1) * rows)
+            left = jnp.concatenate([key_proj[h], inputs], axis=0)
+            for i, block in enumerate((score_grad, attention)):
+                cross[p, i, :, cols] = dot(left, block[:, cols])
+        return jnp.concatenate([score_grad, attention], axis=1)
+
+    def over_heads(block):
+        total = block[:, :rows]
         for h in range(1, sharing):
-            crossed = crossed + dot(key_proj[h], score_grad[:, h * rows : (h + 1) * rows])
-        acc_q[query_at] += crossed
-        return dot_nt(score_grad, projected[0]) + dot_nt(attention_low, projected[1])
+            total = total + block[:, h * rows : (h + 1) * rows]
+        return total
+
+    def settle(cross, p, shares, mine, keep, projected, at):
+        scale, centre = shares
+        grown = scale * mine[1] * keep
+        moved = grown * (mine[2] / mine[1] - centre)
+        low, even = cross[p, 0], cross[p, 1]
+        acc_q[at] += over_heads(low[:R_OUT] * grown + even[:R_OUT] * moved)
+        span = sharing * rows
+        by_query, by_out = projected[:, :span].astype(F32), projected[:, span:].astype(F32)
+        left = jnp.concatenate([by_query * grown, by_query * moved + by_out * grown], axis=1)
+        sums = jnp.concatenate([low[R_OUT:], even[R_OUT:]], axis=1)
+        grad_rest[at] += dot_nt(left.astype(BF16), sums.astype(BF16))
 
     def queries_of(g):
         many = columns(g, wide)
@@ -939,7 +984,7 @@
         weight = wq_ref[:, columns(b, wide)]
         for h, block in enumerate(key_projection(weight, keys_b)):
             home_proj[p, h] = block
-        row_proj[p, 2], row_proj[p, 3] = project(b, query, grad_out)
+        row_proj[p, 1] = project(b, query, grad_out)
         query, grad_out = queries_of(a)
         keys = jnp.concatenate([near[p, 0], keys_a], axis=0)
         values = jnp.concatenate([near[p, 1], values_a], axis=0)
@@ -947,7 +992,7 @@
         weight = wq_ref[:, columns(a, wide)]
         for h, block in enumerate(key_projection(weight, keys)):
             near_proj[p, h] = block
-        row_proj[p, 0], row_proj[p, 1] = project(a, query, grad_out)
+        row_proj[p, 0] = project(a, query, grad_out)
 
     def second(p):
         a, b = 2 * p, 2 * p + 1
@@ -978,6 +1023,21 @@
             rest_copy(p).start()
 
         many_a, many_b = columns(a, wide), columns(b, wide)
+        weight = jnp.where(carried, wq_ref[:, many_a], wq_ref[:, many_b])
+        far_proj = key_projection(weight, far[p, 0])
+        home_keys = [home_proj[p, h] for h in range(sharing)]
+        mine = rows_of(next_stats, p)
+        scale = 1.0 / mine[1]
+        prepare(
+            next_work,
+            p,
+            (scale, mine[2] * scale),
+            [jnp.concatenate([far_proj[h], home_keys[h]], axis=1) for h in range(sharing)],
+            rows,
+            next_cross,
+            p,
+        )
+        next_proj[p] = project(b, by_head(following[p, 0]), by_head(following[p, 1]))
         query = by_head(jnp.where(carried, q_buf[:, many_a], q_buf[:, many_b]))
         grad_out = by_head(jnp.where(carried, o_buf[:, many_a], o_buf[:, many_b]))
         forward(
@@ -987,61 +1047,51 @@
         home = rows_of(home_stats, p)
         far_rows = rows_of(far_stats, p)
         none = (jnp.full_like(mine[0], 2 * NEG_FILL), jnp.zeros_like(mine[1]), jnp.zeros_like(mine[2]))
-        acc_kv[rows : 3 * rows] += backward(
+        acc_kv[:, rows : 3 * rows] += backward(
             near_work,
             p,
             share(mine, choose(far_rows, none)),
             [near_proj[p, h] for h in range(sharing)],
-            (row_proj[p, 0], row_proj[p, 1]),
+            row_proj[p, 0],
             0,
         )
-        weight = jnp.where(carried, wq_ref[:, many_a], wq_ref[:, many_b])
-        far_proj = key_projection(weight, far[p, 0])
         acc_far[...] += backward(
             far_work,
             0,
             share(far_rows, choose(mine, home)),
             far_proj,
-            choose((row_proj[p, 0], row_proj[p, 1]), (row_proj[p, 2], row_proj[p, 3])),
+            jnp.where(carried, row_proj[p, 0], row_proj[p, 1]),
             0,
         )
-        for h, block in enumerate(far_proj):
-            near_proj[p, h, :, :rows] = block
-
-    def third(p):
-        b = 2 * p + 1
-        projected = project(b, by_head(following[p, 0]), by_head(following[p, 1]))
-
-        @pl.when(has_left)
-        def _():
-            rest_copy(p).wait_recv()
-
-        @pl.when(has_right)
-        def _():
-            home_copy(p).wait_recv()
-
-        home = rows_of(home_stats, p)
-        home_keys = [home_proj[p, h] for h in range(sharing)]
-        acc_kv[2 * rows : 3 * rows] += backward(
+        both = prepare(
             home_work,
             p,
-            share(home, choose(rows_of(home_rest, p), rows_of(far_stats, p))),
+            share(home, choose(none, far_rows)),
             home_keys,
-            (row_proj[p, 2], row_proj[p, 3]),
-            0,
-        )
-        key_proj = [
-            jnp.concatenate([near_proj[p, h, :, :rows], home_keys[h]], axis=1)
-            for h in range(sharing)
-        ]
-        acc_kv[rows : 3 * rows] += backward(
-            next_work,
+            2 * rows,
+            home_cross,
             p,
-            share(rows_of(next_stats, p), rows_of(next_rest, p)),
-            key_proj,
-            projected,
-            1,
-        )
+        )
+        keep = 1.0 - crossing[0:1]
+        acc_q[0] += over_heads(home_cross[p, 0, :R_OUT] * keep)
+        kept = row_proj[p, 1].astype(F32) * jnp.concatenate([keep, keep], axis=1)
+        acc_kv[:, 2 * rows : 3 * rows] += dot_nt(kept.astype(BF16), both)
+
+    def third(p):
+        @pl.when(has_left)
+        def _():
+            rest_copy(p).wait_recv()
+
+        @pl.when(has_right)
+        def _():
+            home_copy(p).wait_recv()
+
+        mine = rows_of(next_stats, p)
+        shares = share(mine, rows_of(next_rest, p))
+        settle(next_cross, p, shares, mine, 1.0, next_proj[p], 1)
+        mine = rows_of(home_stats, p)
+        shares = share(mine, rows_of(home_rest, p))
+        settle(home_cross, p, shares, mine, crossing[0:1], row_proj[p, 1], 0)
 
     chosen = index_ref[...]
     tests = own_scores.shape[1]
@@ -1058,14 +1108,6 @@
             first(it)
             lax.fori_loop(it * n_all // pairs, (it + 1) * n_all // pairs, build, 0)
 
-        @pl.when((it > 0) & (it <= pairs))
-        def _():
-            second(it - 1)
-
-        @pl.when(it > 1)
-        def _():
-            third(it - 2)
-
         @pl.when(it == 1)
         def _():
             @pl.when(has_left)
@@ -1076,6 +1118,14 @@
             def _():
                 x_copy(1).start()
 
+        @pl.when((it > 0) & (it <= pairs))
+        def _():
+            second(it - 1)
+
+        @pl.when(it > 1)
+        def _():
+            third(it - 2)
+
         @pl.when(it == jnp.minimum(seq, steps - 1))
         def _():
             @pl.when(has_left)
@@ -1108,9 +1158,9 @@
     def _():
         x_copy(2).wait_recv()
 
-    acc_kv[:rows] += jnp.where(carried, acc_far[...], 0.0)
-    acc_kv[rows : 2 * rows] += jnp.where(carried, 0.0, acc_far[...])
-    projected = acc_kv[...].T + jnp.concatenate(
+    acc_kv[:, :rows] += jnp.where(carried, acc_far[...], 0.0)
+    acc_kv[:, rows : 2 * rows] += jnp.where(carried, 0.0, acc_far[...])
+    projected = acc_kv[...] + jnp.concatenate(
         [jnp.zeros((R_OUT, 2 * rows), F32), acc_q[0], acc_q[1]], axis=1
     )
     inputs = x_buf[...]
@@ -1120,6 +1170,9 @@
         [jnp.where(key_doc == d, projected, 0.0) for d in range(DOCS)], axis=0
     )
     spread[...] = dot_nt(marked.astype(BF16), inputs).reshape(spread.shape)
+    after, before = doc_at(start + rows - 1), doc_at(start)
+    for d in range(DOCS):
+        spread[d] += jnp.where(after == d, grad_rest[1], 0.0) + jnp.where(before == d, grad_rest[0], 0.0)
     width = part.shape[2]
     for o in range(R_OUT):
         column = o * R_IN
@@ -1148,31 +1201,43 @@
     parts.wait_recv()
     red_low[...] = jnp.sum(red_in[...].astype(F32), axis=0).astype(BF16)
 
-    slot = doc * n_red + red
+    plane = n_doc * n_head
 
     def send_low(j, carry):
         place = device_of((me + j) % n_all)
-        block_copy(red_low, low_all.at[slot], send2, recv2, place).start()
+        block_copy(red_low, low_all.at[me], send2, recv2.at[seq], place).start()
         return carry
 
     lax.fori_loop(1, n_all, send_low, 0)
-    low_all[slot] = red_low[...]
+    low_all[me] = red_low[...]
     local_copies[-1].wait()
-    others = low_all.at[pl.ds(0, n_all - 1)]
-    lows = block_copy(others, others, send2, recv2, device_of(me))
-    lows.wait_recv()
+
+    def by_distance(i):
+        if n_seq != 4:
+            return (seq + i) % n_seq
+        nearest = 1 + seq % 2
+        farthest = 3 * (1 - seq // 2)
+        return (nearest, 6 - seq - nearest - farthest, farthest)[i - 1]
+
+    def arrived(blocks, send, recv, place, count):
+        others = blocks.at[pl.ds(0, count)]
+        block_copy(others, others, send, recv.at[place], device_of(me)).wait_recv()
 
     local = jnp.zeros(own_scores.shape, F32)
-    for i in range(n_red):
-        low_ref[:, i * width : (i + 1) * width] = low_all[doc * n_red + i]
-        block = jnp.concatenate(
-            [low_all[d * n_red + i].astype(F32) for d in range(n_doc)], axis=0
-        ).astype(BF16)
-        local = local + dot_nt(block, test_buf[:, i * width : (i + 1) * width])
+    for i in range(n_seq):
+        place = by_distance(i) if i else seq
+        if i or plane > 1:
+            arrived(low_all, send2, recv2, place, plane if i else plane - 1)
+        for h in range(n_head):
+            at = pl.ds(pl.multiple_of((place * n_head + h) * width, width), width)
+            low_ref[:, at] = low_all[(place * n_doc + doc) * n_head + h]
+            block = jnp.concatenate(
+                [low_all[(place * n_doc + d) * n_head + h].astype(F32) for d in range(n_doc)],
+                axis=0,
+            ).astype(BF16)
+            local = local + dot_nt(block, test_buf[:, at])
     out_copies[0].start()
     own_scores[...] = local.astype(BF16)
-
-    plane = n_doc * n_head
 
     def score_copy(peer):
         return block_copy(
@@ -1193,13 +1258,11 @@
         return dot(several, hot[pl.ds(place * plane, plane)].reshape(plane * tests, -1))
 
     if plane > 1:
-        others = score_all.at[pl.ds(0, plane - 1)]
-        block_copy(others, others, send3, recv3.at[seq], device_of(me)).wait_recv()
+        arrived(score_all, send3, recv3, seq, plane - 1)
     total = select(seq)
-    others = score_all.at[pl.ds(0, plane)]
     for i in range(1, n_seq):
-        place = (seq + i) % n_seq
-        block_copy(others, others, send3, recv3.at[place], device_of(me)).wait_recv()
+        place = by_distance(i)
+        arrived(score_all, send3, recv3, place, plane)
         total = total + select(place)
     scores_ref[...] = total
     out_copies[1].start()
@@ -1222,7 +1285,8 @@
         x_copy(1).wait_send()
 
     parts.wait_send()
-    lows.wait_send()
+    others = low_all.at[pl.ds(0, n_all - 1)]
+    block_copy(others, others, send2, recv2.at[0], device_of(me)).wait_send()
     others = score_all.at[pl.ds(0, n_all - 1)]
     block_copy(others, others, send3, recv3.at[0], device_of(me)).wait_send()
     for copy in out_copies:
@@ -1344,7 +1408,12 @@
         pltpu.VMEM((pairs, 2, 2 * rows, stacked), F32),
         pltpu.VMEM((pairs, span // HDIM, R_OUT, 2 * rows), BF16),
         pltpu.VMEM((pairs, span // HDIM, R_OUT, rows), BF16),
-        pltpu.VMEM((pairs, 4, R_OUT, stacked), BF16),
+        pltpu.VMEM((pairs, 2, R_OUT, 2 * stacked), BF16),
+        pltpu.VMEM((pairs, 2, R_OUT + R_IN, stacked), F32),
+        pltpu.VMEM((pairs, 2, R_OUT + R_IN, stacked), F32),
+        pltpu.VMEM((pairs, R_OUT, 2 * stacked), BF16),
+        pltpu.VMEM((2, R_OUT, R_IN), F32),
+        pltpu.VMEM((8, stacked), F32),
         stats,
         stats,
         stats,
@@ -1352,8 +1421,8 @@
         stats,
         stats,
         pltpu.VMEM((2, R_OUT, rows), F32),
-        pltpu.VMEM((4 * rows, R_OUT), F32),
-        pltpu.VMEM((rows, R_OUT), F32),
+        pltpu.VMEM((R_OUT, 4 * rows), F32),
+        pltpu.VMEM((R_OUT, rows), F32),
         pltpu.VMEM((DOCS, R_OUT, R_IN), F32),
         pltpu.VMEM((n_red, DOCS, width), BF16),
         pltpu.VMEM((n_red, DOCS, width), BF16),
@@ -1378,7 +1447,7 @@
         dma(()),
         dma(()),
         dma(()),
-        dma(()),
+        dma((n_seq,)),
         dma(()),
         dma((n_seq,)),
         pltpu.SemaphoreType.REGULAR,

time: 54.9 us -> 53.8 us (0.980)
  Pallas kernels: 54.1 us -> 53 us
    pallas_call x1, Pallas kernels: 52.6 us -> 51.5 us  [body(): pl.pallas_call(work, out_shape=(jax.ShapeDtypeStruct((DOCS, R_OUT * R_IN)...]
where the time goes in v6:
time: 53.8 us; the launch traced here: 53.7 us
  Pallas kernels  53 us (99%)
  between operations  0.64 us (1%)
    pallas_call x1, Pallas kernels, body(): pl.pallas_call(work, out_shape=(jax.ShapeDtypeStruct((DOCS, R_OUT * R_IN)...  51.5 us
    pallas_call x1, Pallas kernels, body(): pl.pallas_call(hand_over, out_shape=(jax.ShapeDtypeStruct(doc_low.shape,...  1.52 us

profile of v6, /device:TPU:0, one launch (start us, length us, event | category | flops | bytes accessed | tf_op | source)
XLA Modules:
  0.0 53.7 jit_solution(1516420233858168962)
XLA Ops:
  0.6 51.5 %shard_map.113 = (bf16[8,4096]{1,0:T(8,128)(2,1)}, f32[16,1024]{1,0:T(8,128)}) custom-call(s32[1,8]{1,0:T(1,128)} %lengths_hbm.1, bf16[1,256,2048]{2,1,0:T(8,128)(2,1)} %q_hbm.1, bf16[1,256,2048]{2,1,0:T(8,128)(2,1)} %out_hbm.1, bf16[1,256,1024]{2,1,0:T(8,128)(2,1)} %k_hbm.1, bf16[1,256,1024]{2,1,0:T(8,128)(2,1)} %v_hbm.1, bf16[64,256]{1,0:T(8,128)(2,1)} %bitcast.8, ...), custom_call_target="tpu_custom_call" | custom-call | tf_op jit(solution)/shard_map/pallas_call | solution.py:1462
  52.2 1.5 %shard_map.114 = (bf16[8,4096]{1,0:T(8,128)(2,1)}, f32[16,1024]{1,0:T(8,128)}) custom-call(bf16[8,4096]{1,0:T(8,128)(2,1)} %get-tuple-element.4.low_in, f32[16,1024]{1,0:T(8,128)} %get-tuple-element.5.scores_in), custom_call_target="tpu_custom_call" | custom-call | tf_op jit(solution)/shard_map/pallas_call | solution.py:1497

commit v7 on v6

--- a/solution.py
+++ b/solution.py
@@ -1166,10 +1166,10 @@
     inputs = x_buf[...]
     key_pos = start - 2 * rows + lax.broadcasted_iota(jnp.int32, (1, 4 * rows), 1)
     key_doc = doc_numbers(key_pos, ends)
-    marked = jnp.concatenate(
-        [jnp.where(key_doc == d, projected, 0.0) for d in range(DOCS)], axis=0
-    )
-    spread[...] = dot_nt(marked.astype(BF16), inputs).reshape(spread.shape)
+    low_projected = projected.astype(BF16)
+    for d in range(DOCS):
+        mark = jnp.where(key_doc == d, 1.0, 0.0).astype(BF16)
+        spread[d] = dot_nt(low_projected * mark, inputs)
     after, before = doc_at(start + rows - 1), doc_at(start)
     for d in range(DOCS):
         spread[d] += jnp.where(after == d, grad_rest[1], 0.0) + jnp.where(before == d, grad_rest[0], 0.0)
@@ -1252,10 +1252,11 @@
     score_all[me] = local.astype(BF16)
 
     def select(place):
-        several = jnp.concatenate(
-            [score_all[place * plane + i].astype(F32) for i in range(plane)], axis=1
-        ).astype(BF16)
-        return dot(several, hot[pl.ds(place * plane, plane)].reshape(plane * tests, -1))
+        total = 0.0
+        for i in range(plane):
+            peer = place * plane + i
+            total = total + dot(score_all[peer], hot[peer])
+        return total
 
     if plane > 1:
         arrived(score_all, send3, recv3, seq, plane - 1)

time: 53.8 us -> 53.3 us (level)
  Pallas kernels: 53 us -> 52.4 us
    pallas_call x1, Pallas kernels: 51.5 us -> 50.9 us  [body(): pl.pallas_call(work, out_shape=(jax.ShapeDtypeStruct((DOCS, R_OUT * R_IN)...]
where the time goes in v7:
time: 53.3 us; the launch traced here: 53.1 us
  Pallas kernels  52.4 us (98%)
  between operations  0.64 us (1%)
    pallas_call x1, Pallas kernels, body(): pl.pallas_call(work, out_shape=(jax.ShapeDtypeStruct((DOCS, R_OUT * R_IN)...  50.9 us
    pallas_call x1, Pallas kernels, body(): pl.pallas_call(hand_over, out_shape=(jax.ShapeDtypeStruct(doc_low.shape,...  1.52 us

profile of v7, /device:TPU:0, one launch (start us, length us, event | category | flops | bytes accessed | tf_op | source)
XLA Modules:
  0.0 53.1 jit_solution(12139793243527101566)
XLA Ops:
  0.6 50.9 %shard_map.113 = (bf16[8,4096]{1,0:T(8,128)(2,1)}, f32[16,1024]{1,0:T(8,128)}) custom-call(s32[1,8]{1,0:T(1,128)} %lengths_hbm.1, bf16[1,256,2048]{2,1,0:T(8,128)(2,1)} %q_hbm.1, bf16[1,256,2048]{2,1,0:T(8,128)(2,1)} %out_hbm.1, bf16[1,256,1024]{2,1,0:T(8,128)(2,1)} %k_hbm.1, bf16[1,256,1024]{2,1,0:T(8,128)(2,1)} %v_hbm.1, bf16[64,256]{1,0:T(8,128)(2,1)} %bitcast.8, ...), custom_call_target="tpu_custom_call" | custom-call | tf_op jit(solution)/shard_map/pallas_call | solution.py:1463
  51.6 1.5 %shard_map.114 = (bf16[8,4096]{1,0:T(8,128)(2,1)}, f32[16,1024]{1,0:T(8,128)}) custom-call(bf16[8,4096]{1,0:T(8,128)(2,1)} %get-tuple-element.4.low_in, f32[16,1024]{1,0:T(8,128)} %get-tuple-element.5.scores_in), custom_call_target="tpu_custom_call" | custom-call | tf_op jit(solution)/shard_map/pallas_call | solution.py:1498
